TPU v7x, 128 devices: a whole 4x4x4 slice. The times are simulated.
128 devices in a mesh: dp: 16 (over x_hi, y, core), section: 8 (over x_lo, z).
Axes of the slice: x: 4 (x_hi: 2, x_lo: 2; x = x_hi * 2 + x_lo), y: 4, z: 4, core: 2. Of those that a mesh axis runs over, the one named last changes fastest.
Arguments:
- inputs: bfloat16 [2560, 8192], P('dp'), may hold values from -6 to 6
- cotangent: bfloat16 [2560, 8192], P('dp'), may hold values from -0.4375 to 0.4375
- weight_in: bfloat16 [8, 8192, 512], P('section'), may hold values from -0.0625 to 0.0625
- weight_out: bfloat16 [8, 8192, 512], P('section'), may hold values from -0.25 to 0.25
- norm_gains: float32 [8, 8192], P('section'), may hold values from 0.1 to 1.9
Outputs:
- in_grad: float32 [8, 8192, 512], P('section', 'dp')
- out_grad: float32 [8, 8192, 512], P('section', 'dp')
- gain_grad: float32 [8, 8192], P('section', 'dp')
All inputs are finite; a program needn't handle non-finite values.
Results may differ from a plain program's by a relative error of at most 0.025.
Values may be sent and summed in bfloat16 or wider, within the bound.
No kernel may reach another device: no remote copies, remote signals or barrier semaphores. Data moves between devices by JAX's collectives and lax.ppermute only.
A program may use at most 192 MiB of HBM per device.

v0:
```python
import functools

import jax
import jax.numpy as jnp
from jax import lax
from jax.experimental import pallas as pl
from jax.experimental.pallas import tpu as pltpu
from jax.sharding import Mesh
from jax.sharding import PartitionSpec as P

ROWS = 16
WAIT = 2
FIRST, SECOND = 4, 8
ROWS_AT = (7, 7, 7, 6, 6, 6, 5, 5)
FIRST_AT = (5, 5, 4, 4, 4, 3, 3, 3)
SECOND_AT = (2, 2, 2, 2, 1, 1, 1, 1)
UNROLL = 8
FLIP = 2
SCOPED = 6 << 20
DP = ("dp_0", "dp_1", "dp_2")
CHIPS = ("dp_0", "dp_1")
CORE = "dp_2"
EPSILON = 1e-05

VMEM = pl.BlockSpec(memory_space=pltpu.VMEM)
SMEM = pl.BlockSpec(memory_space=pltpu.SMEM)
HBM = pl.BlockSpec(memory_space=pltpu.HBM)


def bring_in(low, micro, mine, came_ref, source_ref, rows_ref, sem):
    def fetch():
        copy = pltpu.make_async_copy(source_ref.at[pl.ds(low * ROWS, ROWS), :], rows_ref, sem)
        copy.start()
        copy.wait()

    if came_ref is None:
        fetch()
    elif not 0 <= low < micro:
        rows_ref[...] = came_ref[...]
    else:
        pl.when(mine)(fetch)

        @pl.when(jnp.logical_not(mine))
        def _():
            rows_ref[...] = came_ref[...]


def turned(k, ctl_ref):
    return jnp.bitwise_xor(ctl_ref[ctl_ref.shape[0] - 3], k)


def column_cut(k, size):
    return pl.ds(pl.multiple_of(k * size, size), size)


def forward_body(tick, micro, skipped, flipped, *refs):
    starting = tick == 0
    ctl_ref, source_ref, w_in_far, w_out_far, gain_ref, *refs = refs
    came_ref = None if starting else refs[0]
    (out_ref, rows_all, pre_all, w_in_ref, w_out_ref, rows_ref, source_sem, load_sem) = refs[-8:]
    width, hidden = w_in_ref.shape
    pieces, _, _, size = rows_all.shape
    slot = ctl_ref[tick]

    def load(which, k):
        far, near = ((w_in_far, w_in_ref), (w_out_far, w_out_ref))[which]
        cut = column_cut(k, size)
        return pltpu.make_async_copy(far.at[cut, :], near.at[cut, :], load_sem.at[which, k])

    if starting:
        for which in range(2):
            for k in range(pieces):
                load(which, k).start()
    mine = ctl_ref[ctl_ref.shape[0] - 2] == 1
    bring_in(tick, micro, mine, came_ref, source_ref, rows_ref, source_sem)

    def project(k, carry):
        pre, total = carry
        if starting:
            load(0, k).wait()
        cut = column_cut(k, size)
        rows = rows_ref[:, cut]
        rows_all[turned(k, ctl_ref), slot] = rows
        rows = rows.astype(jnp.float32)
        pre = pre + jnp.dot(
            (rows * gain_ref[:, cut]).astype(jnp.bfloat16), w_in_ref[cut, :], preferred_element_type=jnp.float32
        )
        return pre, total + jnp.sum(rows * rows, axis=1, keepdims=True)

    zeros = jnp.zeros((ROWS, hidden), jnp.float32), jnp.zeros((ROWS, 1), jnp.float32)
    pre, total = lax.fori_loop(0, pieces, project, zeros, unroll=UNROLL)
    row_scale = lax.rsqrt(total / width + EPSILON)
    pre = pre * row_scale
    pre_all[slot, :, :hidden] = pre
    pre_all[slot, :, hidden:] = jnp.broadcast_to(row_scale, (ROWS, 128))
    act = (pre * jax.nn.sigmoid(pre)).astype(jnp.bfloat16)
    if skipped:
        return

    def expand(k, carry):
        if starting:
            load(1, k).wait()
        cut = column_cut(k, size)
        if flipped:
            branch = jnp.dot(act, w_out_ref[:, cut], preferred_element_type=jnp.float32)
        else:
            branch = lax.dot_general(
                act, w_out_ref[cut, :], (((1,), (1,)), ((), ())), preferred_element_type=jnp.float32
            )
        out_ref[:, cut] = (rows_ref[:, cut].astype(jnp.float32) + branch).astype(jnp.bfloat16)
        return carry

    lax.fori_loop(0, pieces, expand, 0, unroll=UNROLL)


def forward_step(tick, micro, skipped, flipped, pieces, ctl, source, w_in, w_out, gain, came, stores):
    width, hidden = w_in.shape
    starting = tick == 0
    weight = HBM if starting else VMEM
    return pl.pallas_call(
        functools.partial(forward_body, tick, micro, skipped, flipped),
        out_shape=(
            jax.ShapeDtypeStruct((ROWS, width), jnp.bfloat16),
            pltpu.VMEM((pieces, micro + 1, ROWS, width // pieces), jnp.bfloat16),
            pltpu.VMEM((micro + 1, ROWS, hidden + 128), jnp.float32),
            pltpu.VMEM(w_in.shape, jnp.bfloat16),
            pltpu.VMEM(w_out.shape, jnp.bfloat16),
        ),
        in_specs=[SMEM, HBM, weight, weight, VMEM] + [VMEM] * (0 if starting else 3),
        out_specs=(VMEM,) * 5,
        scratch_shapes=[
            pltpu.VMEM((ROWS, width), jnp.bfloat16),
            pltpu.SemaphoreType.DMA,
            pltpu.SemaphoreType.DMA((2, pieces)),
        ],
        input_output_aliases={} if starting else {2: 3, 3: 4, 6: 1, 7: 2},
        compiler_params=pltpu.CompilerParams(vmem_limit_bytes=SCOPED),
        name="forward_step",
    )(ctl, source, w_in, w_out, gain, *(() if starting else (came, *stores)))


def flip_body(far_ref, near_ref, flat_ref):
    for low in range(0, far_ref.shape[0], 512):
        flat_ref[:, low : low + 512] = jnp.transpose(near_ref[low : low + 512, :])


def flip(weight):
    return pl.pallas_call(
        flip_body,
        out_shape=(pltpu.VMEM(weight.shape, weight.dtype), pltpu.VMEM(weight.shape[::-1], weight.dtype)),
        in_specs=[VMEM],
        out_specs=(VMEM, VMEM),
        input_output_aliases={0: 0},
        cost_estimate=pl.CostEstimate(flops=5_000_000_000, transcendentals=0, bytes_accessed=16_000_000),
        compiler_params=pltpu.CompilerParams(vmem_limit_bytes=SCOPED),
        name="flip",
    )(weight)


def backward_body(tick, micro, last, *refs):
    ends = micro + 2 * last - 1
    starting = tick == last
    ctl_ref, source_ref, w_in_in, w_out_in, gain_ref, rows_in, pre_in, *refs = refs
    came_ref = None if starting else refs[0]
    (out_ref, rows_all, pre_all, up_all, pair_all, w_in_ref, w_out_ref, up_ref, sem) = refs[-9:]
    width, hidden = w_out_ref.shape
    pieces, _, _, size = rows_all.shape
    slot = ctl_ref[micro + tick]
    mine = ctl_ref[ctl_ref.shape[0] - 1] == 1
    bring_in(tick - last, micro, mine, came_ref, source_ref, up_ref, sem)

    def project(k, total):
        cut = column_cut(k, size)
        up = up_ref[:, cut]
        up_all[turned(k, ctl_ref), slot] = up
        return total + jnp.dot(up, w_out_ref[cut, :], preferred_element_type=jnp.float32)

    grad_act = lax.fori_loop(0, pieces, project, jnp.zeros((ROWS, hidden), jnp.float32), unroll=UNROLL)
    pre = pre_all[slot, :, :hidden]
    row_scale = pre_all[slot, :, hidden : hidden + 1]
    sig = jax.nn.sigmoid(pre)
    grad_pre = grad_act * sig * (1.0 + pre * (1.0 - sig))
    scaled = (grad_pre * row_scale).astype(jnp.bfloat16)
    pair_all[slot, :, :hidden] = scaled
    pair_all[slot, :, hidden:] = (pre * sig).astype(jnp.bfloat16)
    if tick == ends:
        return
    pull = jnp.sum(scaled.astype(jnp.float32) * pre, axis=1, keepdims=True) * row_scale / width

    def expand(k, carry):
        cut = column_cut(k, size)
        grad_norm = jnp.dot(scaled, w_in_ref[:, cut], preferred_element_type=jnp.float32)
        out_ref[:, cut] = (
            up_ref[:, cut].astype(jnp.float32)
            + grad_norm * gain_ref[:, cut]
            - rows_all[turned(k, ctl_ref), slot].astype(jnp.float32) * pull
        ).astype(jnp.bfloat16)
        return carry

    lax.fori_loop(0, pieces, expand, 0, unroll=UNROLL)


def backward_step(tick, micro, last, pieces, ctl, source, w_in, w_out, gain, stores, came, kept):
    width, hidden = w_out.shape
    starting = tick == last
    size = width // pieces
    return pl.pallas_call(
        functools.partial(backward_body, tick, micro, last),
        out_shape=(
            jax.ShapeDtypeStruct((ROWS, width), jnp.bfloat16),
            pltpu.VMEM((pieces, micro + 1, ROWS, size), jnp.bfloat16),
            pltpu.VMEM((micro + 1, ROWS, hidden + 128), jnp.float32),
            pltpu.VMEM((pieces, micro + 1, ROWS, size), jnp.bfloat16),
            pltpu.VMEM((micro + 1, ROWS, 2 * hidden), jnp.bfloat16),
            pltpu.VMEM(w_in.shape, jnp.bfloat16),
            pltpu.VMEM(w_out.shape, jnp.bfloat16),
        ),
        in_specs=[SMEM, HBM] + [VMEM] * (5 if starting else 8),
        out_specs=(VMEM,) * 7,
        scratch_shapes=[pltpu.VMEM((ROWS, width), jnp.bfloat16), pltpu.SemaphoreType.DMA],
        input_output_aliases={2: 5, 3: 6, 5: 1, 6: 2, **({} if starting else {8: 3, 9: 4})},
        compiler_params=pltpu.CompilerParams(vmem_limit_bytes=SCOPED),
        name="backward_step",
    )(ctl, source, w_in, w_out, gain, *stores, *(() if starting else (came, *kept)))


def gradient_body(plan, counts, ctl_ref, *refs):
    adding, splitting = counts
    sources = 1 + max(entry[0] for entry in plan)
    sources, refs = refs[:sources], refs[sources:]
    *bufs, sems = refs[-4:]
    copies = [
        pltpu.make_async_copy(sources[k].at[pl.ds(low, size), :], bufs[which].at[pl.ds(at, size), :], sems.at[n])
        for n, (k, low, size, which, at) in enumerate(plan)
    ]
    for copy in copies:
        copy.start()
    for copy in copies:
        copy.wait()
    rows_buf, up_buf, pair_buf = bufs
    size = rows_buf.shape[1]
    hidden = pair_buf.shape[1] // 2
    core = ctl_ref[ctl_ref.shape[0] - 4]

    def product(left, right):
        return lax.dot_general(left, right, (((0,), (0,)), ((), ())), preferred_element_type=jnp.float32)

    half = size // 2
    for which in range(2):
        low = pl.multiple_of((core if which == 0 else 1 - core) * half, half) if splitting else which * half
        rows = rows_buf[:, pl.ds(low, half)]
        ups = up_buf[:, pl.ds(low, half)]
        for side, value in enumerate(
            (product(rows, pair_buf[:, :hidden]), product(ups, pair_buf[:, hidden:]))
        ):
            at = slice(side * hidden, (side + 1) * hidden)
            if adding:
                value = value + refs[0][pl.ds(low, half), at]
            if splitting:
                out_ref = refs[adding + which]
                out_ref[:, at] = value.astype(out_ref.dtype)
            else:
                refs[adding][pl.ds(low, half), at] = value


def gradient_step(ctl, groups, sent, span, before, splitting):
    low, high = span
    plan, sources = [], []
    for name, content in groups.items():
        used = False
        for d, piece in enumerate(sent[name]):
            base = 0
            for kind, first, stop in content:
                start, end = max(first, low), min(stop, high)
                if start < end:
                    at = (d * (high - low) + start - low) * ROWS
                    plan.append((len(sources) + d, base + (start - first) * ROWS, (end - start) * ROWS, kind, at))
                    used = True
                base += (stop - first) * ROWS
        if used:
            sources += sent[name]
    size = sources[0].shape[1]
    tokens = (high - low) * ROWS * len(sent[name])
    if splitting:
        out_shape = (
            jax.ShapeDtypeStruct((size // 2, size), jnp.float32),
            jax.ShapeDtypeStruct((size // 2, size), jnp.bfloat16),
        )
    else:
        out_shape = (jax.ShapeDtypeStruct((size, size), jnp.float32),)
    adding = 0 if before is None else 1
    return pl.pallas_call(
        functools.partial(gradient_body, tuple(plan), (adding, splitting)),
        out_shape=out_shape,
        in_specs=[SMEM] + [pl.BlockSpec(memory_space=pl.ANY)] * len(sources) + [VMEM] * adding,
        out_specs=(VMEM,) * len(out_shape),
        scratch_shapes=[pltpu.VMEM((tokens, size), jnp.bfloat16)] * 3 + [pltpu.SemaphoreType.DMA((len(plan),))],
        compiler_params=pltpu.CompilerParams(vmem_limit_bytes=20 << 20),
        name="gradient_step",
    )(ctl, *sources, *(() if before is None else (before,)))


def finish_body(mine_ref, came_ref, w_ref, gain_ref, in_ref, out_ref, sum_ref):
    hidden = in_ref.shape[1]
    total = mine_ref[...] + came_ref[...].astype(jnp.float32)
    plain = total[:, :hidden]
    in_ref[...] = plain * gain_ref[:, :1]
    out_ref[...] = total[:, hidden:]
    ones = jnp.ones((8, hidden), jnp.float32)
    sum_ref[...] = lax.dot_general(
        ones,
        plain * w_ref[...].astype(jnp.float32),
        (((1,), (1,)), ((), ())),
        precision=lax.Precision.HIGHEST,
        preferred_element_type=jnp.float32,
    )[:1]


def local(inputs, cotangent, weight_in, weight_out, norm_gains):
    gain = norm_gains
    tokens, width = inputs.shape
    hidden = weight_in.shape[2]
    micro = tokens // ROWS
    sections = lax.axis_size("section")
    last = sections - 1
    pos = lax.axis_index("section")
    chips = lax.axis_size(CHIPS)
    half = width // (chips * lax.axis_size(CORE))
    onward = [(i, (i + 1) % sections) for i in range(sections)]
    back = [((i + 1) % sections, i) for i in range(sections)]
    ticks = jnp.arange(micro + last)
    which = jnp.concatenate([ticks - pos, ticks - last + pos])
    slots = jnp.where((which >= 0) & (which < micro), which, micro)
    own = jnp.stack([lax.axis_index(CORE), lax.axis_index(CHIPS), pos == 0, pos == last])
    ctl = jnp.concatenate([slots, own]).astype(jnp.int32)
    low = lax.axis_index(DP) * half
    gain_cut = jnp.broadcast_to(lax.dynamic_slice_in_dim(gain[0], low, half, 0)[:, None], (half, 128))
    w_cut = lax.dynamic_slice_in_dim(weight_in[0], low, half, 0)
    ctl, gain_cut, w_cut, inputs, cotangent, w_in_near, w_out_near = lax.optimization_barrier(
        (ctl, gain_cut, w_cut, inputs, cotangent, weight_in[0], weight_out[0])
    )
    inputs, cotangent, w_in_near, w_out_near = (
        pltpu.with_memory_space_constraint(array, pltpu.HBM)
        for array in (inputs, cotangent, w_in_near, w_out_near)
    )

    def shift(tile, d):
        tile = tile.reshape(-1, tile.shape[-1])
        return lax.ppermute(tile, CHIPS, [(i, i ^ d) for i in range(chips)]) if d else tile

    groups = {
        "rows": ((0, 0, micro),),
        "first": ((1, 0, FIRST), (2, 0, FIRST)),
        "second": ((1, FIRST, SECOND), (2, FIRST, SECOND)),
        "third": ((1, SECOND, micro), (2, SECOND, micro)),
    }
    sent = {name: [None] * chips for name in groups}
    leaving = {}
    end = micro + 2 * last - 1
    for name, when in (
        ("rows", ROWS_AT),
        ("first", FIRST_AT),
        ("second", SECOND_AT),
        ("third", (0,) * chips),
    ):
        for d, back_by in enumerate(when):
            leaving.setdefault(end - back_by, []).append((name, d))

    stores = kept = came = arriving = None
    for tick in range(micro + 2 * last):
        if tick < micro + last:
            flipped = tick >= FLIP
            out = w_out_flat if flipped else w_out_near
            made, *stores, w_in_near, out = forward_step(
                tick, micro, tick == micro + last - 1, flipped, chips, ctl, inputs, w_in_near, out, gain, came, stores
            )
            if flipped:
                w_out_flat = out
            else:
                w_out_near = out
            came = lax.ppermute(made, "section", onward)
            if tick == FLIP - 2:
                w_out_near, w_out_flat = flip(w_out_near)
            if tick == FLIP - 1:
                w_in_near, w_in_flat = flip(w_in_near)
        due = leaving.get(tick - WAIT, ()) if tick >= last else ()
        if due:
            arriving, *pieces = lax.optimization_barrier((arriving, *(sent[name][d] for name, d in due)))
            for (name, d), piece in zip(due, pieces):
                sent[name][d] = piece
        if tick >= last:
            made, *both, w_in_flat, w_out_near = backward_step(
                tick, micro, last, chips, ctl, cotangent, w_in_flat, w_out_near, gain, stores, arriving, kept
            )
            stores, kept = both[:2], both[2:]
            if tick < end:
                arriving = lax.ppermute(made, "section", back)
            for name, d in leaving.get(tick, ()):
                sources = (stores[0][d], kept[0][d], kept[1])
                tiles = [sources[kind][low:high] for kind, low, high in groups[name]]
                sent[name][d] = shift(jnp.concatenate(tiles) if len(tiles) > 1 else tiles[0], d)
    (before,) = gradient_step(ctl, groups, sent, (0, SECOND), None, False)
    mine, theirs = gradient_step(ctl, groups, sent, (SECOND, micro), before, True)
    theirs = lax.ppermute(theirs, CORE, [(0, 1), (1, 0)])
    in_grad, out_grad, gain_grad = pl.pallas_call(
        finish_body,
        out_shape=(
            jax.ShapeDtypeStruct((half, hidden), jnp.float32),
            jax.ShapeDtypeStruct((half, hidden), jnp.float32),
            jax.ShapeDtypeStruct((1, half), jnp.float32),
        ),
        in_specs=[VMEM] * 4,
        out_specs=(VMEM,) * 3,
        compiler_params=pltpu.CompilerParams(vmem_limit_bytes=12 << 20),
        name="finish",
    )(mine, theirs, w_cut, gain_cut)
    return (in_grad[None], out_grad[None], gain_grad)


def solution(mesh):
    finer = Mesh(
        mesh.devices.reshape(2, 4, 2, mesh.shape["section"]), ("dp_0", "dp_1", "dp_2", "section")
    )
    in_specs = (
        P(DP, None),
        P(DP, None),
        P("section", None, None),
        P("section", None, None),
        P("section", None),
    )
    out_specs = (P("section", DP, None), P("section", DP, None), P("section", DP))
    return jax.shard_map(local, mesh=finer, in_specs=in_specs, out_specs=out_specs, check_vma=False)
```

profile of v0, /device:TPU:1, one launch (start us, length us, event | category | flops | bytes accessed | tf_op | source)
XLA Modules:
  0.0 387.9 jit_solution(4120803179509520443)
XLA Ops:
  3.5 10.9 %forward_step.17 = (bf16[16,8192]{1,0:T(8,128)(2,1)S(1)}, bf16[8,11,16,1024]{3,2,1,0:T(8,128)(2,1)S(1)}, f32[11,16,640]{2,1,0:T(8,128)S(1)}, bf16[8192,512]{1,0:T(8,128)(2,1)S(1)}, bf16[8192,512]{1,0:T(8,128)(2,1)S(1)}) custom-call(s32[38]{0:T(128)S(1)} %concatenate.79.refs_0_.ctl_ref, bf16[160,8192]{1,0:T(8,128)(2,1)} %refs_1_.25, ...), custom_call_target="tpu_custom_call" | custom-call | tf_op jit(solution)/shard_map/forward_step/pallas_call | solution.py:120
  19.4 6.7 %collective-permute-done.refs_5_ = bf16[16,8192]{1,0:T(8,128)(2,1)S(1)} collective-permute-done((bf16[16,8192]{1,0:T(8,128)(2,1)S(1)}, bf16[16,8192]{1,0:T(8,128)(2,1)S(1)}, u32[]{:S(2)}, u32[]{:S(2)}) %collective-permute-start) | collective-permute-done | bytes 262176 | tf_op jit(solution)/shard_map/ppermute | solution.py:381
  26.1 5.1 %forward_step.18 = (bf16[16,8192]{1,0:T(8,128)(2,1)S(1)}, bf16[8,11,16,1024]{3,2,1,0:T(8,128)(2,1)S(1)}, f32[11,16,640]{2,1,0:T(8,128)S(1)}, bf16[8192,512]{1,0:T(8,128)(2,1)S(1)}, bf16[8192,512]{1,0:T(8,128)(2,1)S(1)}) custom-call(s32[38]{0:T(128)S(1)} %concatenate.79.refs_0_.ctl_ref, ...), custom_call_target="tpu_custom_call", output_to_operand_aliasing={{3}: (2, {}), {4}: (3, {}), {1}: (6, {}), {2}: (7, {})} | custom-call | tf_op jit(solution)/shard_map/forward_step/pallas_call | solution.py:120
  33.7 6.2 %collective-permute-done.1.refs_5_ = bf16[16,8192]{1,0:T(8,128)(2,1)S(1)} collective-permute-done((bf16[16,8192]{1,0:T(8,128)(2,1)S(1)}, bf16[16,8192]{1,0:T(8,128)(2,1)S(1)}, u32[]{:S(2)}, u32[]{:S(2)}) %collective-permute-start.1) | collective-permute-done | bytes 262176 | tf_op jit(solution)/shard_map/ppermute | solution.py:381
  44.1 7.7 %collective-permute-done.2.refs_5_ = bf16[16,8192]{1,0:T(8,128)(2,1)S(1)} collective-permute-done((bf16[16,8192]{1,0:T(8,128)(2,1)S(1)}, bf16[16,8192]{1,0:T(8,128)(2,1)S(1)}, u32[]{:S(2)}, u32[]{:S(2)}) %collective-permute-start.2) | collective-permute-done | bytes 262176 | tf_op jit(solution)/shard_map/ppermute | solution.py:381
  51.8 4.5 %forward_step.20 = (bf16[16,8192]{1,0:T(8,128)(2,1)S(1)}, bf16[8,11,16,1024]{3,2,1,0:T(8,128)(2,1)S(1)}, f32[11,16,640]{2,1,0:T(8,128)S(1)}, bf16[8192,512]{1,0:T(8,128)(2,1)S(1)}, bf16[512,8192]{1,0:T(8,128)(2,1)S(1)}) custom-call(s32[38]{0:T(128)S(1)} %concatenate.79.refs_0_.ctl_ref, ...), custom_call_target="tpu_custom_call", output_to_operand_aliasing={{3}: (2, {}), {4}: (3, {}), {1}: (6, {}), {2}: (7, {})} | custom-call | tf_op jit(solution)/shard_map/forward_step/pallas_call | solution.py:120
  56.4 7.3 %collective-permute-done.3.refs_5_ = bf16[16,8192]{1,0:T(8,128)(2,1)S(1)} collective-permute-done((bf16[16,8192]{1,0:T(8,128)(2,1)S(1)}, bf16[16,8192]{1,0:T(8,128)(2,1)S(1)}, u32[]{:S(2)}, u32[]{:S(2)}) %collective-permute-start.3) | collective-permute-done | bytes 262176 | tf_op jit(solution)/shard_map/ppermute | solution.py:381
  63.7 4.0 %forward_step.21 = (bf16[16,8192]{1,0:T(8,128)(2,1)S(1)}, bf16[8,11,16,1024]{3,2,1,0:T(8,128)(2,1)S(1)}, f32[11,16,640]{2,1,0:T(8,128)S(1)}, bf16[8192,512]{1,0:T(8,128)(2,1)S(1)}, bf16[512,8192]{1,0:T(8,128)(2,1)S(1)}) custom-call(s32[38]{0:T(128)S(1)} %concatenate.79.refs_0_.ctl_ref, ...), custom_call_target="tpu_custom_call", output_to_operand_aliasing={{3}: (2, {}), {4}: (3, {}), {1}: (6, {}), {2}: (7, {})} | custom-call | tf_op jit(solution)/shard_map/forward_step/pallas_call | solution.py:120
  67.8 7.3 %collective-permute-done.4.refs_5_ = bf16[16,8192]{1,0:T(8,128)(2,1)S(1)} collective-permute-done((bf16[16,8192]{1,0:T(8,128)(2,1)S(1)}, bf16[16,8192]{1,0:T(8,128)(2,1)S(1)}, u32[]{:S(2)}, u32[]{:S(2)}) %collective-permute-start.4) | collective-permute-done | bytes 262176 | tf_op jit(solution)/shard_map/ppermute | solution.py:381
  75.1 4.0 %forward_step.22 = (bf16[16,8192]{1,0:T(8,128)(2,1)S(1)}, bf16[8,11,16,1024]{3,2,1,0:T(8,128)(2,1)S(1)}, f32[11,16,640]{2,1,0:T(8,128)S(1)}, bf16[8192,512]{1,0:T(8,128)(2,1)S(1)}, bf16[512,8192]{1,0:T(8,128)(2,1)S(1)}) custom-call(s32[38]{0:T(128)S(1)} %concatenate.79.refs_0_.ctl_ref, ...), custom_call_target="tpu_custom_call", output_to_operand_aliasing={{3}: (2, {}), {4}: (3, {}), {1}: (6, {}), {2}: (7, {})} | custom-call | tf_op jit(solution)/shard_map/forward_step/pallas_call | solution.py:120
  79.3 7.3 %collective-permute-done.5.refs_5_ = bf16[16,8192]{1,0:T(8,128)(2,1)S(1)} collective-permute-done((bf16[16,8192]{1,0:T(8,128)(2,1)S(1)}, bf16[16,8192]{1,0:T(8,128)(2,1)S(1)}, u32[]{:S(2)}, u32[]{:S(2)}) %collective-permute-start.5) | collective-permute-done | bytes 262176 | tf_op jit(solution)/shard_map/ppermute | solution.py:381
  90.7 7.3 %collective-permute-done.6.refs_5_ = bf16[16,8192]{1,0:T(8,128)(2,1)S(1)} collective-permute-done((bf16[16,8192]{1,0:T(8,128)(2,1)S(1)}, bf16[16,8192]{1,0:T(8,128)(2,1)S(1)}, u32[]{:S(2)}, u32[]{:S(2)}) %collective-permute-start.6) | collective-permute-done | bytes 262176 | tf_op jit(solution)/shard_map/ppermute | solution.py:381
  109.9 4.0 %forward_step.25 = (bf16[16,8192]{1,0:T(8,128)(2,1)S(1)}, bf16[8,11,16,1024]{3,2,1,0:T(8,128)(2,1)S(1)}, f32[11,16,640]{2,1,0:T(8,128)S(1)}, bf16[8192,512]{1,0:T(8,128)(2,1)S(1)}, bf16[512,8192]{1,0:T(8,128)(2,1)S(1)}) custom-call(s32[38]{0:T(128)S(1)} %concatenate.79.refs_0_.ctl_ref, ...), custom_call_target="tpu_custom_call", output_to_operand_aliasing={{3}: (2, {}), {4}: (3, {}), {1}: (6, {}), {2}: (7, {})} | custom-call | tf_op jit(solution)/shard_map/forward_step/pallas_call | solution.py:120
  117.0 4.5 %collective-permute-start.10 = (bf16[16,8192]{1,0:T(8,128)(2,1)S(1)}, bf16[16,8192]{1,0:T(8,128)(2,1)S(1)}, u32[]{:S(2)}, u32[]{:S(2)}) collective-permute-start(bf16[16,8192]{1,0:T(8,128)(2,1)S(1)} %get-tuple-element.308), channel_id=1, source_target_pairs={{1,0},{2,1},{3,2},{4,3},{5,4},{6,5},{7,6},{0,7},{9,8},{10,9},{11,1... | collective-permute-start | bytes 786440 | tf_op jit(solution)/shard_map/ppermute | solution.py:397
  121.5 4.0 %forward_step.26 = (bf16[16,8192]{1,0:T(8,128)(2,1)S(1)}, bf16[8,11,16,1024]{3,2,1,0:T(8,128)(2,1)S(1)}, f32[11,16,640]{2,1,0:T(8,128)S(1)}, bf16[8192,512]{1,0:T(8,128)(2,1)S(1)}, bf16[512,8192]{1,0:T(8,128)(2,1)S(1)}) custom-call(s32[38]{0:T(128)S(1)} %concatenate.79.refs_0_.ctl_ref, ...), custom_call_target="tpu_custom_call", output_to_operand_aliasing={{3}: (2, {}), {4}: (3, {}), {1}: (6, {}), {2}: (7, {})} | custom-call | tf_op jit(solution)/shard_map/forward_step/pallas_call | solution.py:120
  128.7 4.8 %collective-permute-start.12 = (bf16[16,8192]{1,0:T(8,128)(2,1)S(1)}, bf16[16,8192]{1,0:T(8,128)(2,1)S(1)}, u32[]{:S(2)}, u32[]{:S(2)}) collective-permute-start(bf16[16,8192]{1,0:T(8,128)(2,1)S(1)} %get-tuple-element.320), channel_id=1, source_target_pairs={{1,0},{2,1},{3,2},{4,3},{5,4},{6,5},{7,6},{0,7},{9,8},{10,9},{11,1... | collective-permute-start | bytes 786440 | tf_op jit(solution)/shard_map/ppermute | solution.py:397
  140.0 5.0 %collective-permute-start.14 = (bf16[16,8192]{1,0:T(8,128)(2,1)S(1)}, bf16[16,8192]{1,0:T(8,128)(2,1)S(1)}, u32[]{:S(2)}, u32[]{:S(2)}) collective-permute-start(bf16[16,8192]{1,0:T(8,128)(2,1)S(1)} %get-tuple-element.332), channel_id=1, source_target_pairs={{1,0},{2,1},{3,2},{4,3},{5,4},{6,5},{7,6},{0,7},{9,8},{10,9},{11,1... | collective-permute-start | bytes 786440 | tf_op jit(solution)/shard_map/ppermute | solution.py:397
  152.9 5.0 %collective-permute-start.16 = (bf16[16,8192]{1,0:T(8,128)(2,1)S(1)}, bf16[16,8192]{1,0:T(8,128)(2,1)S(1)}, u32[]{:S(2)}, u32[]{:S(2)}) collective-permute-start(bf16[16,8192]{1,0:T(8,128)(2,1)S(1)} %get-tuple-element.344), channel_id=1, source_target_pairs={{1,0},{2,1},{3,2},{4,3},{5,4},{6,5},{7,6},{0,7},{9,8},{10,9},{11,1... | collective-permute-start | bytes 786440 | tf_op jit(solution)/shard_map/ppermute | solution.py:397
  167.4 5.3 %collective-permute-start.18 = (bf16[16,8192]{1,0:T(8,128)(2,1)S(1)}, bf16[16,8192]{1,0:T(8,128)(2,1)S(1)}, u32[]{:S(2)}, u32[]{:S(2)}) collective-permute-start(bf16[16,8192]{1,0:T(8,128)(2,1)S(1)} %get-tuple-element.356), channel_id=1, source_target_pairs={{1,0},{2,1},{3,2},{4,3},{5,4},{6,5},{7,6},{0,7},{9,8},{10,9},{11,1... | collective-permute-start | bytes 786440 | tf_op jit(solution)/shard_map/ppermute | solution.py:397
  181.4 5.3 %collective-permute-start.20 = (bf16[16,8192]{1,0:T(8,128)(2,1)S(1)}, bf16[16,8192]{1,0:T(8,128)(2,1)S(1)}, u32[]{:S(2)}, u32[]{:S(2)}) collective-permute-start(bf16[16,8192]{1,0:T(8,128)(2,1)S(1)} %get-tuple-element.368), channel_id=1, source_target_pairs={{1,0},{2,1},{3,2},{4,3},{5,4},{6,5},{7,6},{0,7},{9,8},{10,9},{11,1... | collective-permute-start | bytes 786440 | tf_op jit(solution)/shard_map/ppermute | solution.py:397
  194.1 5.5 %collective-permute-start.22 = (bf16[16,8192]{1,0:T(8,128)(2,1)S(1)}, bf16[16,8192]{1,0:T(8,128)(2,1)S(1)}, u32[]{:S(2)}, u32[]{:S(2)}) collective-permute-start(bf16[16,8192]{1,0:T(8,128)(2,1)S(1)} %get-tuple-element.380), channel_id=1, source_target_pairs={{1,0},{2,1},{3,2},{4,3},{5,4},{6,5},{7,6},{0,7},{9,8},{10,9},{11,1... | collective-permute-start | bytes 786440 | tf_op jit(solution)/shard_map/ppermute | solution.py:397
  206.2 5.3 %collective-permute-start.24 = (bf16[16,8192]{1,0:T(8,128)(2,1)S(1)}, bf16[16,8192]{1,0:T(8,128)(2,1)S(1)}, u32[]{:S(2)}, u32[]{:S(2)}) collective-permute-start(bf16[16,8192]{1,0:T(8,128)(2,1)S(1)} %get-tuple-element.392), channel_id=1, source_target_pairs={{1,0},{2,1},{3,2},{4,3},{5,4},{6,5},{7,6},{0,7},{9,8},{10,9},{11,1... | collective-permute-start | bytes 786440 | tf_op jit(solution)/shard_map/ppermute | solution.py:397
  217.8 5.0 %collective-permute-start.25 = (bf16[16,8192]{1,0:T(8,128)(2,1)S(1)}, bf16[16,8192]{1,0:T(8,128)(2,1)S(1)}, u32[]{:S(2)}, u32[]{:S(2)}) collective-permute-start(bf16[16,8192]{1,0:T(8,128)(2,1)S(1)} %get-tuple-element.399), channel_id=1, source_target_pairs={{1,0},{2,1},{3,2},{4,3},{5,4},{6,5},{7,6},{0,7},{9,8},{10,9},{11,1... | collective-permute-start | bytes 786440 | tf_op jit(solution)/shard_map/ppermute | solution.py:397
  245.0 4.9 %collective-permute-start.34 = (bf16[160,1024]{1,0:T(8,128)(2,1)S(1)}, bf16[160,1024]{1,0:T(8,128)(2,1)S(1)}, u32[]{:S(2)}, u32[]{:S(2)}) collective-permute-start(bf16[160,1024]{1,0:T(8,128)(2,1)S(1)} %bitcast.99), channel_id=1, source_target_pairs={{0,96},{16,112},{32,64},{48,80},{64,32},{80,48},{96,0},{112,16},{1... | collective-permute-start | bytes 983048 | tf_op jit(solution)/shard_map/ppermute | solution.py:349
  268.6 4.2 %collective-permute-start.37 = (bf16[16,8192]{1,0:T(8,128)(2,1)S(1)}, bf16[16,8192]{1,0:T(8,128)(2,1)S(1)}, u32[]{:S(2)}, u32[]{:S(2)}) collective-permute-start(bf16[16,8192]{1,0:T(8,128)(2,1)S(1)} %get-tuple-element.438), channel_id=1, source_target_pairs={{1,0},{2,1},{3,2},{4,3},{5,4},{6,5},{7,6},{0,7},{9,8},{10,9},{11,1... | collective-permute-start | bytes 786440 | tf_op jit(solution)/shard_map/ppermute | solution.py:397
  281.9 4.4 %collective-permute-start.41 = (bf16[16,8192]{1,0:T(8,128)(2,1)S(1)}, bf16[16,8192]{1,0:T(8,128)(2,1)S(1)}, u32[]{:S(2)}, u32[]{:S(2)}) collective-permute-start(bf16[16,8192]{1,0:T(8,128)(2,1)S(1)} %get-tuple-element.446), channel_id=1, source_target_pairs={{1,0},{2,1},{3,2},{4,3},{5,4},{6,5},{7,6},{0,7},{9,8},{10,9},{11,1... | collective-permute-start | bytes 786440 | tf_op jit(solution)/shard_map/ppermute | solution.py:397
  288.8 4.7 %collective-permute-done.44.refs_15_ = bf16[128,1024]{1,0:T(8,128)(2,1)S(1)} collective-permute-done((bf16[128,1024]{1,0:T(8,128)(2,1)S(1)}, bf16[128,1024]{1,0:T(8,128)(2,1)S(1)}, u32[]{:S(2)}, u32[]{:S(2)}) %collective-permute-start.44) | collective-permute-done | bytes 262176 | tf_op jit(solution)/shard_map/ppermute | solution.py:349
  297.7 4.3 %collective-permute-done.41.refs_7_ = bf16[16,8192]{1,0:T(8,128)(2,1)S(1)} collective-permute-done((bf16[16,8192]{1,0:T(8,128)(2,1)S(1)}, bf16[16,8192]{1,0:T(8,128)(2,1)S(1)}, u32[]{:S(2)}, u32[]{:S(2)}) %collective-permute-start.41) | collective-permute-done | bytes 262176 | tf_op jit(solution)/shard_map/ppermute | solution.py:397
  305.0 4.1 %collective-permute-start.45 = (bf16[16,8192]{1,0:T(8,128)(2,1)S(1)}, bf16[16,8192]{1,0:T(8,128)(2,1)S(1)}, u32[]{:S(2)}, u32[]{:S(2)}) collective-permute-start(bf16[16,8192]{1,0:T(8,128)(2,1)S(1)} %get-tuple-element.454), channel_id=1, source_target_pairs={{1,0},{2,1},{3,2},{4,3},{5,4},{6,5},{7,6},{0,7},{9,8},{10,9},{11,1... | collective-permute-start | bytes 786440 | tf_op jit(solution)/shard_map/ppermute | solution.py:397
  329.1 6.1 %collective-permute-done.58.refs_22_ = bf16[128,1024]{1,0:T(8,128)(2,1)S(1)} collective-permute-done((bf16[128,1024]{1,0:T(8,128)(2,1)S(1)}, bf16[128,1024]{1,0:T(8,128)(2,1)S(1)}, u32[]{:S(2)}, u32[]{:S(2)}) %collective-permute-start.58) | collective-permute-done | bytes 262176 | tf_op jit(solution)/shard_map/ppermute | solution.py:349
  344.7 8.9 %gradient_step.2.refs_16_ = f32[1024,1024]{1,0:T(8,128)S(1)} custom-call(s32[38]{0:T(128)S(1)} %concatenate.79.refs_0_.ctl_ref, bf16[160,1024]{1,0:T(8,128)(2,1)S(1)} %bitcast.91, bf16[160,1024]{1,0:T(8,128)(2,1)S(1)} %collective-permute-done.27.refs_1_, bf16[160,1024]{1,0:T(8,128)(2,1)S(1)} %collective-permute-done.28.refs_2_, ...), custom_call_target="tpu_custom_call" | custom-call | tf_op jit(solution)/shard_map/gradient_step/pallas_call | solution.py:292
  357.4 25.6 %collective-permute-start.60 = (bf16[512,1024]{1,0:T(8,128)(2,1)S(1)}, bf16[512,1024]{1,0:T(8,128)(2,1)S(1)}, u32[]{:S(2)}, u32[]{:S(2)}) collective-permute-start(bf16[512,1024]{1,0:T(8,128)(2,1)S(1)} %get-tuple-element.473), channel_id=1, source_target_pairs={{0,8},{8,0},{1,9},{9,1},{2,10},{10,2},{3,11},{11,3},{4,12},{12,4},... | collective-permute-start | bytes 3145736 | tf_op jit(solution)/shard_map/ppermute | solution.py:404
  (160 shorter events, 186.6 us)
Async XLA Ops:
  14.4 11.6 %collective-permute-start = (bf16[16,8192]{1,0:T(8,128)(2,1)S(1)}, bf16[16,8192]{1,0:T(8,128)(2,1)S(1)}, u32[]{:S(2)}, u32[]{:S(2)}) collective-permute-start(bf16[16,8192]{1,0:T(8,128)(2,1)S(1)} %get-tuple-element.249), channel_id=1, source_target_pairs={{0,1},{1,2},{2,3},{3,4},{4,5},{5,6},{6,7},{7,0},{8,9},{9,10},{10,1... | collective-permute-start | bytes 786440 | tf_op jit(solution)/shard_map/ppermute | solution.py:381
  222.9 14.4 %collective-permute-start.27 = (bf16[160,1024]{1,0:T(8,128)(2,1)S(1)}, bf16[160,1024]{1,0:T(8,128)(2,1)S(1)}, u32[]{:S(2)}, u32[]{:S(2)}) collective-permute-start(bf16[160,1024]{1,0:T(8,128)(2,1)S(1)} %bitcast.104), channel_id=1, source_target_pairs={{0,16},{16,0},{32,48},{48,32},{64,80},{80,64},{96,112},{112,96},{1... | collective-permute-start | bytes 983048 | tf_op jit(solution)/shard_map/ppermute | solution.py:349
  224.3 15.1 %collective-permute-start.28 = (bf16[160,1024]{1,0:T(8,128)(2,1)S(1)}, bf16[160,1024]{1,0:T(8,128)(2,1)S(1)}, u32[]{:S(2)}, u32[]{:S(2)}) collective-permute-start(bf16[160,1024]{1,0:T(8,128)(2,1)S(1)} %bitcast.103), channel_id=1, source_target_pairs={{0,32},{16,48},{32,0},{48,16},{64,96},{80,112},{96,64},{112,80},{1... | collective-permute-start | bytes 983048 | tf_op jit(solution)/shard_map/ppermute | solution.py:349
  233.2 11.8 %collective-permute-start.31 = (bf16[160,1024]{1,0:T(8,128)(2,1)S(1)}, bf16[160,1024]{1,0:T(8,128)(2,1)S(1)}, u32[]{:S(2)}, u32[]{:S(2)}) collective-permute-start(bf16[160,1024]{1,0:T(8,128)(2,1)S(1)} %bitcast.102), channel_id=1, source_target_pairs={{0,64},{16,80},{32,96},{48,112},{64,0},{80,16},{96,32},{112,48},{1... | collective-permute-start | bytes 983048 | tf_op jit(solution)/shard_map/ppermute | solution.py:349
  235.8 14.5 %collective-permute-start.32 = (bf16[160,1024]{1,0:T(8,128)(2,1)S(1)}, bf16[160,1024]{1,0:T(8,128)(2,1)S(1)}, u32[]{:S(2)}, u32[]{:S(2)}) collective-permute-start(bf16[160,1024]{1,0:T(8,128)(2,1)S(1)} %bitcast.101), channel_id=1, source_target_pairs={{0,80},{16,64},{32,112},{48,96},{64,16},{80,0},{96,48},{112,32},{1... | collective-permute-start | bytes 983048 | tf_op jit(solution)/shard_map/ppermute | solution.py:349
  237.3 15.2 %collective-permute-start.30 = (bf16[160,1024]{1,0:T(8,128)(2,1)S(1)}, bf16[160,1024]{1,0:T(8,128)(2,1)S(1)}, u32[]{:S(2)}, u32[]{:S(2)}) collective-permute-start(bf16[160,1024]{1,0:T(8,128)(2,1)S(1)} %bitcast.100), channel_id=1, source_target_pairs={{0,48},{16,32},{32,16},{48,0},{64,112},{80,96},{96,80},{112,64},{1... | collective-permute-start | bytes 983048 | tf_op jit(solution)/shard_map/ppermute | solution.py:349
  243.6 15.5 %collective-permute-start.36 = (bf16[128,1024]{1,0:T(8,128)(2,1)S(1)}, bf16[128,1024]{1,0:T(8,128)(2,1)S(1)}, u32[]{:S(2)}, u32[]{:S(2)}) collective-permute-start(bf16[128,1024]{1,0:T(8,128)(2,1)S(1)} %bitcast.110), channel_id=1, source_target_pairs={{0,16},{16,0},{32,48},{48,32},{64,80},{80,64},{96,112},{112,96},{1... | collective-permute-start | bytes 786440 | tf_op jit(solution)/shard_map/ppermute | solution.py:349
  245.0 16.5 %collective-permute-start.34 = (bf16[160,1024]{1,0:T(8,128)(2,1)S(1)}, bf16[160,1024]{1,0:T(8,128)(2,1)S(1)}, u32[]{:S(2)}, u32[]{:S(2)}) collective-permute-start(bf16[160,1024]{1,0:T(8,128)(2,1)S(1)} %bitcast.99), channel_id=1, source_target_pairs={{0,96},{16,112},{32,64},{48,80},{64,32},{80,48},{96,0},{112,16},{1... | collective-permute-start | bytes 983048 | tf_op jit(solution)/shard_map/ppermute | solution.py:349
  250.2 13.8 %collective-permute-start.35 = (bf16[160,1024]{1,0:T(8,128)(2,1)S(1)}, bf16[160,1024]{1,0:T(8,128)(2,1)S(1)}, u32[]{:S(2)}, u32[]{:S(2)}) collective-permute-start(bf16[160,1024]{1,0:T(8,128)(2,1)S(1)} %bitcast.98), channel_id=1, source_target_pairs={{0,112},{16,96},{32,80},{48,64},{64,48},{80,32},{96,16},{112,0},{1... | collective-permute-start | bytes 983048 | tf_op jit(solution)/shard_map/ppermute | solution.py:349
  256.3 19.4 %collective-permute-start.39 = (bf16[128,1024]{1,0:T(8,128)(2,1)S(1)}, bf16[128,1024]{1,0:T(8,128)(2,1)S(1)}, u32[]{:S(2)}, u32[]{:S(2)}) collective-permute-start(bf16[128,1024]{1,0:T(8,128)(2,1)S(1)} %bitcast.111), channel_id=1, source_target_pairs={{0,48},{16,32},{32,16},{48,0},{64,112},{80,96},{96,80},{112,64},{1... | collective-permute-start | bytes 786440 | tf_op jit(solution)/shard_map/ppermute | solution.py:349
  259.1 17.7 %collective-permute-start.40 = (bf16[128,1024]{1,0:T(8,128)(2,1)S(1)}, bf16[128,1024]{1,0:T(8,128)(2,1)S(1)}, u32[]{:S(2)}, u32[]{:S(2)}) collective-permute-start(bf16[128,1024]{1,0:T(8,128)(2,1)S(1)} %bitcast.108), channel_id=1, source_target_pairs={{0,64},{16,80},{32,96},{48,112},{64,0},{80,16},{96,32},{112,48},{1... | collective-permute-start | bytes 786440 | tf_op jit(solution)/shard_map/ppermute | solution.py:349
  261.5 16.8 %collective-permute-start.38 = (bf16[128,1024]{1,0:T(8,128)(2,1)S(1)}, bf16[128,1024]{1,0:T(8,128)(2,1)S(1)}, u32[]{:S(2)}, u32[]{:S(2)}) collective-permute-start(bf16[128,1024]{1,0:T(8,128)(2,1)S(1)} %bitcast.106), channel_id=1, source_target_pairs={{0,32},{16,48},{32,0},{48,16},{64,96},{80,112},{96,64},{112,80},{1... | collective-permute-start | bytes 786440 | tf_op jit(solution)/shard_map/ppermute | solution.py:349
  272.9 15.1 %collective-permute-start.43 = (bf16[128,1024]{1,0:T(8,128)(2,1)S(1)}, bf16[128,1024]{1,0:T(8,128)(2,1)S(1)}, u32[]{:S(2)}, u32[]{:S(2)}) collective-permute-start(bf16[128,1024]{1,0:T(8,128)(2,1)S(1)} %bitcast.109), channel_id=1, source_target_pairs={{0,96},{16,112},{32,64},{48,80},{64,32},{80,48},{96,0},{112,16},{1... | collective-permute-start | bytes 786440 | tf_op jit(solution)/shard_map/ppermute | solution.py:349
  275.7 17.8 %collective-permute-start.44 = (bf16[128,1024]{1,0:T(8,128)(2,1)S(1)}, bf16[128,1024]{1,0:T(8,128)(2,1)S(1)}, u32[]{:S(2)}, u32[]{:S(2)}) collective-permute-start(bf16[128,1024]{1,0:T(8,128)(2,1)S(1)} %bitcast.107), channel_id=1, source_target_pairs={{0,112},{16,96},{32,80},{48,64},{64,48},{80,32},{96,16},{112,0},{1... | collective-permute-start | bytes 786440 | tf_op jit(solution)/shard_map/ppermute | solution.py:349
  276.8 20.9 %collective-permute-start.42 = (bf16[128,1024]{1,0:T(8,128)(2,1)S(1)}, bf16[128,1024]{1,0:T(8,128)(2,1)S(1)}, u32[]{:S(2)}, u32[]{:S(2)}) collective-permute-start(bf16[128,1024]{1,0:T(8,128)(2,1)S(1)} %bitcast.105), channel_id=1, source_target_pairs={{0,80},{16,64},{32,112},{48,96},{64,16},{80,0},{96,48},{112,32},{1... | collective-permute-start | bytes 786440 | tf_op jit(solution)/shard_map/ppermute | solution.py:349
  281.9 20.1 %collective-permute-start.41 = (bf16[16,8192]{1,0:T(8,128)(2,1)S(1)}, bf16[16,8192]{1,0:T(8,128)(2,1)S(1)}, u32[]{:S(2)}, u32[]{:S(2)}) collective-permute-start(bf16[16,8192]{1,0:T(8,128)(2,1)S(1)} %get-tuple-element.446), channel_id=1, source_target_pairs={{1,0},{2,1},{3,2},{4,3},{5,4},{6,5},{7,6},{0,7},{9,8},{10,9},{11,1... | collective-permute-start | bytes 786440 | tf_op jit(solution)/shard_map/ppermute | solution.py:397
  286.5 23.4 %collective-permute-start.46 = (bf16[128,1024]{1,0:T(8,128)(2,1)S(1)}, bf16[128,1024]{1,0:T(8,128)(2,1)S(1)}, u32[]{:S(2)}, u32[]{:S(2)}) collective-permute-start(bf16[128,1024]{1,0:T(8,128)(2,1)S(1)} %bitcast.118), channel_id=1, source_target_pairs={{0,16},{16,0},{32,48},{48,32},{64,80},{80,64},{96,112},{112,96},{1... | collective-permute-start | bytes 786440 | tf_op jit(solution)/shard_map/ppermute | solution.py:349
  288.0 24.7 %collective-permute-start.48 = (bf16[128,1024]{1,0:T(8,128)(2,1)S(1)}, bf16[128,1024]{1,0:T(8,128)(2,1)S(1)}, u32[]{:S(2)}, u32[]{:S(2)}) collective-permute-start(bf16[128,1024]{1,0:T(8,128)(2,1)S(1)} %bitcast.117), channel_id=1, source_target_pairs={{0,48},{16,32},{32,16},{48,0},{64,112},{80,96},{96,80},{112,64},{1... | collective-permute-start | bytes 786440 | tf_op jit(solution)/shard_map/ppermute | solution.py:349
  293.5 21.8 %collective-permute-start.47 = (bf16[128,1024]{1,0:T(8,128)(2,1)S(1)}, bf16[128,1024]{1,0:T(8,128)(2,1)S(1)}, u32[]{:S(2)}, u32[]{:S(2)}) collective-permute-start(bf16[128,1024]{1,0:T(8,128)(2,1)S(1)} %bitcast.116), channel_id=1, source_target_pairs={{0,32},{16,48},{32,0},{48,16},{64,96},{80,112},{96,64},{112,80},{1... | collective-permute-start | bytes 786440 | tf_op jit(solution)/shard_map/ppermute | solution.py:349
  305.0 12.7 %collective-permute-start.45 = (bf16[16,8192]{1,0:T(8,128)(2,1)S(1)}, bf16[16,8192]{1,0:T(8,128)(2,1)S(1)}, u32[]{:S(2)}, u32[]{:S(2)}) collective-permute-start(bf16[16,8192]{1,0:T(8,128)(2,1)S(1)} %get-tuple-element.454), channel_id=1, source_target_pairs={{1,0},{2,1},{3,2},{4,3},{5,4},{6,5},{7,6},{0,7},{9,8},{10,9},{11,1... | collective-permute-start | bytes 786440 | tf_op jit(solution)/shard_map/ppermute | solution.py:397
  309.2 12.8 %collective-permute-start.57 = (bf16[128,1024]{1,0:T(8,128)(2,1)S(1)}, bf16[128,1024]{1,0:T(8,128)(2,1)S(1)}, u32[]{:S(2)}, u32[]{:S(2)}) collective-permute-start(bf16[128,1024]{1,0:T(8,128)(2,1)S(1)} %bitcast.115), channel_id=1, source_target_pairs={{0,80},{16,64},{32,112},{48,96},{64,16},{80,0},{96,48},{112,32},{1... | collective-permute-start | bytes 786440 | tf_op jit(solution)/shard_map/ppermute | solution.py:349
  309.8 19.1 %collective-permute-start.59 = (bf16[128,1024]{1,0:T(8,128)(2,1)S(1)}, bf16[128,1024]{1,0:T(8,128)(2,1)S(1)}, u32[]{:S(2)}, u32[]{:S(2)}) collective-permute-start(bf16[128,1024]{1,0:T(8,128)(2,1)S(1)} %bitcast.114), channel_id=1, source_target_pairs={{0,112},{16,96},{32,80},{48,64},{64,48},{80,32},{96,16},{112,0},{1... | collective-permute-start | bytes 786440 | tf_op jit(solution)/shard_map/ppermute | solution.py:349
  312.7 22.5 %collective-permute-start.58 = (bf16[128,1024]{1,0:T(8,128)(2,1)S(1)}, bf16[128,1024]{1,0:T(8,128)(2,1)S(1)}, u32[]{:S(2)}, u32[]{:S(2)}) collective-permute-start(bf16[128,1024]{1,0:T(8,128)(2,1)S(1)} %bitcast.113), channel_id=1, source_target_pairs={{0,96},{16,112},{32,64},{48,80},{64,32},{80,48},{96,0},{112,16},{1... | collective-permute-start | bytes 786440 | tf_op jit(solution)/shard_map/ppermute | solution.py:349
  315.3 22.8 %collective-permute-start.56 = (bf16[128,1024]{1,0:T(8,128)(2,1)S(1)}, bf16[128,1024]{1,0:T(8,128)(2,1)S(1)}, u32[]{:S(2)}, u32[]{:S(2)}) collective-permute-start(bf16[128,1024]{1,0:T(8,128)(2,1)S(1)} %bitcast.112), channel_id=1, source_target_pairs={{0,64},{16,80},{32,96},{48,112},{64,0},{80,16},{96,32},{112,48},{1... | collective-permute-start | bytes 786440 | tf_op jit(solution)/shard_map/ppermute | solution.py:349
  319.5 19.6 %collective-permute-start.49 = (bf16[64,1024]{1,0:T(8,128)(2,1)S(1)}, bf16[64,1024]{1,0:T(8,128)(2,1)S(1)}, u32[]{:S(2)}, u32[]{:S(2)}) collective-permute-start(bf16[64,1024]{1,0:T(8,128)(2,1)S(1)} %bitcast.125), channel_id=1, source_target_pairs={{0,16},{16,0},{32,48},{48,32},{64,80},{80,64},{96,112},{112,96},{1... | collective-permute-start | bytes 393224 | tf_op jit(solution)/shard_map/ppermute | solution.py:349
  322.0 19.2 %collective-permute-start.55 = (bf16[64,1024]{1,0:T(8,128)(2,1)S(1)}, bf16[64,1024]{1,0:T(8,128)(2,1)S(1)}, u32[]{:S(2)}, u32[]{:S(2)}) collective-permute-start(bf16[64,1024]{1,0:T(8,128)(2,1)S(1)} %bitcast.124), channel_id=1, source_target_pairs={{0,112},{16,96},{32,80},{48,64},{64,48},{80,32},{96,16},{112,0},{1... | collective-permute-start | bytes 393224 | tf_op jit(solution)/shard_map/ppermute | solution.py:349
  328.9 24.7 %collective-permute-start.50 = (bf16[64,1024]{1,0:T(8,128)(2,1)S(1)}, bf16[64,1024]{1,0:T(8,128)(2,1)S(1)}, u32[]{:S(2)}, u32[]{:S(2)}) collective-permute-start(bf16[64,1024]{1,0:T(8,128)(2,1)S(1)} %bitcast.123), channel_id=1, source_target_pairs={{0,32},{16,48},{32,0},{48,16},{64,96},{80,112},{96,64},{112,80},{1... | collective-permute-start | bytes 393224 | tf_op jit(solution)/shard_map/ppermute | solution.py:349
  335.2 18.4 %collective-permute-start.51 = (bf16[64,1024]{1,0:T(8,128)(2,1)S(1)}, bf16[64,1024]{1,0:T(8,128)(2,1)S(1)}, u32[]{:S(2)}, u32[]{:S(2)}) collective-permute-start(bf16[64,1024]{1,0:T(8,128)(2,1)S(1)} %bitcast.122), channel_id=1, source_target_pairs={{0,48},{16,32},{32,16},{48,0},{64,112},{80,96},{96,80},{112,64},{1... | collective-permute-start | bytes 393224 | tf_op jit(solution)/shard_map/ppermute | solution.py:349
  338.1 15.6 %collective-permute-start.52 = (bf16[64,1024]{1,0:T(8,128)(2,1)S(1)}, bf16[64,1024]{1,0:T(8,128)(2,1)S(1)}, u32[]{:S(2)}, u32[]{:S(2)}) collective-permute-start(bf16[64,1024]{1,0:T(8,128)(2,1)S(1)} %bitcast.121), channel_id=1, source_target_pairs={{0,64},{16,80},{32,96},{48,112},{64,0},{80,16},{96,32},{112,48},{1... | collective-permute-start | bytes 393224 | tf_op jit(solution)/shard_map/ppermute | solution.py:349
  339.2 14.5 %collective-permute-start.53 = (bf16[64,1024]{1,0:T(8,128)(2,1)S(1)}, bf16[64,1024]{1,0:T(8,128)(2,1)S(1)}, u32[]{:S(2)}, u32[]{:S(2)}) collective-permute-start(bf16[64,1024]{1,0:T(8,128)(2,1)S(1)} %bitcast.120), channel_id=1, source_target_pairs={{0,80},{16,64},{32,112},{48,96},{64,16},{80,0},{96,48},{112,32},{1... | collective-permute-start | bytes 393224 | tf_op jit(solution)/shard_map/ppermute | solution.py:349
  341.2 12.4 %collective-permute-start.54 = (bf16[64,1024]{1,0:T(8,128)(2,1)S(1)}, bf16[64,1024]{1,0:T(8,128)(2,1)S(1)}, u32[]{:S(2)}, u32[]{:S(2)}) collective-permute-start(bf16[64,1024]{1,0:T(8,128)(2,1)S(1)} %bitcast.119), channel_id=1, source_target_pairs={{0,96},{16,112},{32,64},{48,80},{64,32},{80,48},{96,0},{112,16},{1... | collective-permute-start | bytes 393224 | tf_op jit(solution)/shard_map/ppermute | solution.py:349
  357.4 27.9 %collective-permute-start.60 = (bf16[512,1024]{1,0:T(8,128)(2,1)S(1)}, bf16[512,1024]{1,0:T(8,128)(2,1)S(1)}, u32[]{:S(2)}, u32[]{:S(2)}) collective-permute-start(bf16[512,1024]{1,0:T(8,128)(2,1)S(1)} %get-tuple-element.473), channel_id=1, source_target_pairs={{0,8},{8,0},{1,9},{9,1},{2,10},{10,2},{3,11},{11,3},{4,12},{12,4},... | collective-permute-start | bytes 3145736 | tf_op jit(solution)/shard_map/ppermute | solution.py:404
  (31 other events, 275.5 us)
where the time goes:
time: 395 us; the launch traced here: 388 us
  starting transfers between devices  146 us (37%)
  Pallas kernels  139 us (35%)
  waiting for transfers between devices  96.9 us (25%)
    pallas_call x17, Pallas kernels, forward_step(): pl.pallas_call(functools.partial(forward_body, tick, micro, skipped, flip...  69.4 us
    ppermute x16, starting transfers between devices, local(): arriving = lax.ppermute(made, 'section', back)  67.3 us
    ppermute x16, waiting for transfers between devices, local(): came = lax.ppermute(made, 'section', onward)  52.2 us
    pallas_call x17, Pallas kernels, backward_step(): pl.pallas_call(functools.partial(backward_body, tick, micro, last), out_s...  50.2 us
    ppermute x28, starting transfers between devices, shift(): lax.ppermute(tile, CHIPS, [(i, i ^ d) for i in range(chips)])  49.6 us
    ppermute x28, waiting for transfers between devices, shift(): lax.ppermute(tile, CHIPS, [(i, i ^ d) for i in range(chips)])  27.3 us
    ppermute x1, starting transfers between devices, local(): theirs = lax.ppermute(theirs, CORE, [(0, 1), (1, 0)])  25.6 us
    ppermute x16, waiting for transfers between devices, local(): arriving = lax.ppermute(made, 'section', back)  15.1 us
  transfers between devices with their start and end apart: 61, of which 29 were waited for; matrix products, arithmetic and copies ran while one was open for 0% of the time, Pallas kernels for 23%

commit v1 on v0

--- a/solution.py
+++ b/solution.py
@@ -11,15 +11,17 @@
 ROWS = 16
 WAIT = 2
 FIRST, SECOND = 4, 8
-ROWS_AT = (7, 7, 7, 6, 6, 6, 5, 5)
-FIRST_AT = (5, 5, 4, 4, 4, 3, 3, 3)
-SECOND_AT = (2, 2, 2, 2, 1, 1, 1, 1)
+ROWS_AT = (7, 7, 6, 5)
+FIRST_AT = (5, 5, 4, 3)
+SECOND_AT = (2, 2, 2, 1)
 UNROLL = 8
 FLIP = 2
 SCOPED = 6 << 20
 DP = ("dp_0", "dp_1", "dp_2")
 CHIPS = ("dp_0", "dp_1")
 CORE = "dp_2"
+RING = "dp_1"
+FAR = "dp_0"
 EPSILON = 1e-05
 
 VMEM = pl.BlockSpec(memory_space=pltpu.VMEM)
@@ -224,11 +226,11 @@
     )(ctl, source, w_in, w_out, gain, *stores, *(() if starting else (came, *kept)))
 
 
-def gradient_body(plan, counts, ctl_ref, *refs):
-    adding, splitting = counts
-    sources = 1 + max(entry[0] for entry in plan)
-    sources, refs = refs[:sources], refs[sources:]
-    *bufs, sems = refs[-4:]
+def gradient_body(plan, ctl_ref, *refs):
+    count = 1 + max(entry[0] for entry in plan)
+    sources, refs = refs[:count], refs[count:]
+    mine_in, theirs_in, mine_out, theirs_out, rows_buf, up_buf, pair_buf, sems = refs
+    bufs = (rows_buf.at[0], rows_buf.at[1], up_buf.at[0], up_buf.at[1], pair_buf)
     copies = [
         pltpu.make_async_copy(sources[k].at[pl.ds(low, size), :], bufs[which].at[pl.ds(at, size), :], sems.at[n])
         for n, (k, low, size, which, at) in enumerate(plan)
@@ -237,75 +239,63 @@
         copy.start()
     for copy in copies:
         copy.wait()
-    rows_buf, up_buf, pair_buf = bufs
-    size = rows_buf.shape[1]
     hidden = pair_buf.shape[1] // 2
+    half = rows_buf.shape[2] // 2
     core = ctl_ref[ctl_ref.shape[0] - 4]
-
-    def product(left, right):
-        return lax.dot_general(left, right, (((0,), (0,)), ((), ())), preferred_element_type=jnp.float32)
-
-    half = size // 2
-    for which in range(2):
-        low = pl.multiple_of((core if which == 0 else 1 - core) * half, half) if splitting else which * half
-        rows = rows_buf[:, pl.ds(low, half)]
-        ups = up_buf[:, pl.ds(low, half)]
-        for side, value in enumerate(
-            (product(rows, pair_buf[:, :hidden]), product(ups, pair_buf[:, hidden:]))
-        ):
-            at = slice(side * hidden, (side + 1) * hidden)
-            if adding:
-                value = value + refs[0][pl.ds(low, half), at]
-            if splitting:
-                out_ref = refs[adding + which]
-                out_ref[:, at] = value.astype(out_ref.dtype)
-            else:
-                refs[adding][pl.ds(low, half), at] = value
-
-
-def gradient_step(ctl, groups, sent, span, before, splitting):
-    low, high = span
+    for buf, right, outs in (
+        (rows_buf, pair_buf[:, :hidden], (mine_in, theirs_in)),
+        (up_buf, pair_buf[:, hidden:], (mine_out, theirs_out)),
+    ):
+        for which, out_ref in enumerate(outs):
+            low = pl.multiple_of((core if which == 0 else 1 - core) * half, half)
+            for tile in range(2):
+                value = lax.dot_general(
+                    buf[tile, :, pl.ds(low, half)],
+                    right,
+                    (((0,), (0,)), ((), ())),
+                    preferred_element_type=jnp.float32,
+                )
+                out_ref[tile] = value.astype(out_ref.dtype)
+
+
+def gradient_step(ctl, groups, sent, micro):
     plan, sources = [], []
     for name, content in groups.items():
-        used = False
         for d, piece in enumerate(sent[name]):
             base = 0
             for kind, first, stop in content:
-                start, end = max(first, low), min(stop, high)
-                if start < end:
-                    at = (d * (high - low) + start - low) * ROWS
-                    plan.append((len(sources) + d, base + (start - first) * ROWS, (end - start) * ROWS, kind, at))
-                    used = True
-                base += (stop - first) * ROWS
-        if used:
-            sources += sent[name]
+                for tile in range(1 if kind == 2 else 2):
+                    size = (stop - first) * ROWS
+                    plan.append((len(sources) + d, base, size, 2 * kind + tile, (d * micro + first) * ROWS))
+                    base += size
+        sources += sent[name]
     size = sources[0].shape[1]
-    tokens = (high - low) * ROWS * len(sent[name])
-    if splitting:
-        out_shape = (
-            jax.ShapeDtypeStruct((size // 2, size), jnp.float32),
-            jax.ShapeDtypeStruct((size // 2, size), jnp.bfloat16),
+    tokens = micro * ROWS * len(sent[name])
+    pairs = (2, size // 2, size // 2)
+    return pl.pallas_call(
+        functools.partial(gradient_body, tuple(plan)),
+        out_shape=(
+            jax.ShapeDtypeStruct(pairs, jnp.float32),
+            jax.ShapeDtypeStruct(pairs, jnp.bfloat16),
         )
-    else:
-        out_shape = (jax.ShapeDtypeStruct((size, size), jnp.float32),)
-    adding = 0 if before is None else 1
-    return pl.pallas_call(
-        functools.partial(gradient_body, tuple(plan), (adding, splitting)),
-        out_shape=out_shape,
-        in_specs=[SMEM] + [pl.BlockSpec(memory_space=pl.ANY)] * len(sources) + [VMEM] * adding,
-        out_specs=(VMEM,) * len(out_shape),
-        scratch_shapes=[pltpu.VMEM((tokens, size), jnp.bfloat16)] * 3 + [pltpu.SemaphoreType.DMA((len(plan),))],
+        * 2,
+        in_specs=[SMEM] + [pl.BlockSpec(memory_space=pl.ANY)] * len(sources),
+        out_specs=(VMEM,) * 4,
+        scratch_shapes=[
+            pltpu.VMEM((2, tokens, size), jnp.bfloat16),
+            pltpu.VMEM((2, tokens, size), jnp.bfloat16),
+            pltpu.VMEM((tokens, size), jnp.bfloat16),
+            pltpu.SemaphoreType.DMA((len(plan),)),
+        ],
         compiler_params=pltpu.CompilerParams(vmem_limit_bytes=20 << 20),
         name="gradient_step",
-    )(ctl, *sources, *(() if before is None else (before,)))
-
-
-def finish_body(mine_ref, came_ref, w_ref, gain_ref, in_ref, out_ref, sum_ref):
+    )(ctl, *sources)
+
+
+def finish_body(mine_ref, near_ref, far_ref, w_ref, gain_ref, in_ref, sum_ref):
     hidden = in_ref.shape[1]
-    total = mine_ref[...] + came_ref[...].astype(jnp.float32)
-    plain = total[:, :hidden]
+    plain = mine_ref[0] + near_ref[0].astype(jnp.float32) + far_ref[...].astype(jnp.float32)
     in_ref[...] = plain * gain_ref[:, :1]
-    out_ref[...] = total[:, hidden:]
     ones = jnp.ones((8, hidden), jnp.float32)
     sum_ref[...] = lax.dot_general(
         ones,
@@ -326,6 +316,7 @@
     pos = lax.axis_index("section")
     chips = lax.axis_size(CHIPS)
     half = width // (chips * lax.axis_size(CORE))
+    size = width // chips
     onward = [(i, (i + 1) % sections) for i in range(sections)]
     back = [((i + 1) % sections, i) for i in range(sections)]
     ticks = jnp.arange(micro + last)
@@ -344,9 +335,10 @@
         for array in (inputs, cotangent, w_in_near, w_out_near)
     )
 
+    rings = lax.axis_size(RING)
+
     def shift(tile, d):
-        tile = tile.reshape(-1, tile.shape[-1])
-        return lax.ppermute(tile, CHIPS, [(i, i ^ d) for i in range(chips)]) if d else tile
+        return lax.ppermute(tile, RING, [(i, i ^ d) for i in range(rings)]) if d else tile
 
     groups = {
         "rows": ((0, 0, micro),),
@@ -354,14 +346,14 @@
         "second": ((1, FIRST, SECOND), (2, FIRST, SECOND)),
         "third": ((1, SECOND, micro), (2, SECOND, micro)),
     }
-    sent = {name: [None] * chips for name in groups}
+    sent = {name: [None] * rings for name in groups}
     leaving = {}
     end = micro + 2 * last - 1
     for name, when in (
         ("rows", ROWS_AT),
         ("first", FIRST_AT),
         ("second", SECOND_AT),
-        ("third", (0,) * chips),
+        ("third", (0,) * rings),
     ):
         for d, back_by in enumerate(when):
             leaving.setdefault(end - back_by, []).append((name, d))
@@ -396,24 +388,34 @@
             if tick < end:
                 arriving = lax.ppermute(made, "section", back)
             for name, d in leaving.get(tick, ()):
-                sources = (stores[0][d], kept[0][d], kept[1])
-                tiles = [sources[kind][low:high] for kind, low, high in groups[name]]
-                sent[name][d] = shift(jnp.concatenate(tiles) if len(tiles) > 1 else tiles[0], d)
-    (before,) = gradient_step(ctl, groups, sent, (0, SECOND), None, False)
-    mine, theirs = gradient_step(ctl, groups, sent, (SECOND, micro), before, True)
-    theirs = lax.ppermute(theirs, CORE, [(0, 1), (1, 0)])
-    in_grad, out_grad, gain_grad = pl.pallas_call(
+                tiles = []
+                for kind, low, high in groups[name]:
+                    if kind == 2:
+                        tiles.append(kept[1][low:high])
+                    else:
+                        store = kept[0] if kind else stores[0]
+                        tiles += [store[d, low:high], store[d + rings, low:high]]
+                tiles = [tile.reshape(-1, size) for tile in tiles]
+                sent[name][d] = shift(jnp.concatenate(tiles), d)
+    sums = gradient_step(ctl, groups, sent, micro)
+    parts = []
+    for mine, theirs in (sums[:2], sums[2:]):
+        near = lax.ppermute(theirs, CORE, [(0, 1), (1, 0)])
+        far = (mine[1] + near[1].astype(jnp.float32)).astype(jnp.bfloat16)
+        parts.append((mine, near, lax.ppermute(far, FAR, [(0, 1), (1, 0)])))
+    in_grad, gain_grad = pl.pallas_call(
         finish_body,
         out_shape=(
             jax.ShapeDtypeStruct((half, hidden), jnp.float32),
-            jax.ShapeDtypeStruct((half, hidden), jnp.float32),
             jax.ShapeDtypeStruct((1, half), jnp.float32),
         ),
-        in_specs=[VMEM] * 4,
-        out_specs=(VMEM,) * 3,
+        in_specs=[VMEM] * 5,
+        out_specs=(VMEM,) * 2,
         compiler_params=pltpu.CompilerParams(vmem_limit_bytes=12 << 20),
         name="finish",
-    )(mine, theirs, w_cut, gain_cut)
+    )(*parts[0], w_cut, gain_cut)
+    mine, near, far = parts[1]
+    out_grad = mine[0] + near[0].astype(jnp.float32) + far.astype(jnp.float32)
     return (in_grad[None], out_grad[None], gain_grad)
 
 

time: 395 us -> 382 us (0.967)
  starting transfers between devices: 146 us -> 129 us
  waiting for transfers between devices: 96.9 us -> 102 us
    ppermute x29 -> x16, starting transfers between devices: 75.2 us -> 60.8 us  [the longest x12 32 us: shift(): lax.ppermute(tile, RING, [(i, i ^ d) for i in range(rings)])]
    ppermute x29 -> x16, waiting for transfers between devices: 29.6 us -> 33.3 us  [the longest x2 20.7 us: local(): parts.append((mine, near, lax.ppermute(far, FAR, [(0, 1), (1, 0)])))]
    pallas_call x2 -> x1, Pallas kernels: 12.6 us -> 10.5 us  [gradient_step(): pl.pallas_call(functools.partial(gradient_body, tuple(plan)), out_shape=(...]
  transfers between devices with their start and end apart: 61 -> 48, of which waited for: 29 -> 26; matrix products, arithmetic and copies ran while one was open for 0% -> 1% of each run, Pallas kernels for 23% -> 22%
where the time goes in v1:
time: 382 us; the launch traced here: 375 us
  Pallas kernels  137 us (36%)
  starting transfers between devices  129 us (34%)
  waiting for transfers between devices  102 us (27%)
    pallas_call x17, Pallas kernels, forward_step(): pl.pallas_call(functools.partial(forward_body, tick, micro, skipped, flip...  69.4 us
    ppermute x16, starting transfers between devices, local(): arriving = lax.ppermute(made, 'section', back)  64.1 us
    ppermute x16, waiting for transfers between devices, local(): came = lax.ppermute(made, 'section', onward)  52.2 us
    pallas_call x17, Pallas kernels, backward_step(): pl.pallas_call(functools.partial(backward_body, tick, micro, last), out_s...  50.3 us
    ppermute x12, starting transfers between devices, shift(): lax.ppermute(tile, RING, [(i, i ^ d) for i in range(rings)])  32 us
    ppermute x2, starting transfers between devices, local(): near = lax.ppermute(theirs, CORE, [(0, 1), (1, 0)])  24.9 us
    ppermute x2, waiting for transfers between devices, local(): parts.append((mine, near, lax.ppermute(far, FAR, [(0, 1), (1, 0)])))  20.7 us
    ppermute x16, waiting for transfers between devices, local(): arriving = lax.ppermute(made, 'section', back)  16.7 us
  transfers between devices with their start and end apart: 48, of which 26 were waited for; matrix products, arithmetic and copies ran while one was open for 1% of the time, Pallas kernels for 22%

profile of v1, /device:TPU:1, one launch (start us, length us, event | category | flops | bytes accessed | tf_op | source)
XLA Modules:
  0.0 374.8 jit_solution(1741650246251627417)
XLA Ops:
  3.5 10.9 %forward_step.17 = (bf16[16,8192]{1,0:T(8,128)(2,1)S(1)}, bf16[8,11,16,1024]{3,2,1,0:T(8,128)(2,1)S(1)}, f32[11,16,640]{2,1,0:T(8,128)S(1)}, bf16[8192,512]{1,0:T(8,128)(2,1)S(1)}, bf16[8192,512]{1,0:T(8,128)(2,1)S(1)}) custom-call(s32[38]{0:T(128)S(1)} %concatenate.55.refs_0_.ctl_ref, bf16[160,8192]{1,0:T(8,128)(2,1)} %refs_1_.25, ...), custom_call_target="tpu_custom_call" | custom-call | tf_op jit(solution)/shard_map/forward_step/pallas_call | solution.py:122
  19.4 6.7 %collective-permute-done.refs_5_ = bf16[16,8192]{1,0:T(8,128)(2,1)S(1)} collective-permute-done((bf16[16,8192]{1,0:T(8,128)(2,1)S(1)}, bf16[16,8192]{1,0:T(8,128)(2,1)S(1)}, u32[]{:S(2)}, u32[]{:S(2)}) %collective-permute-start) | collective-permute-done | bytes 262176 | tf_op jit(solution)/shard_map/ppermute | solution.py:373
  26.1 5.1 %forward_step.18 = (bf16[16,8192]{1,0:T(8,128)(2,1)S(1)}, bf16[8,11,16,1024]{3,2,1,0:T(8,128)(2,1)S(1)}, f32[11,16,640]{2,1,0:T(8,128)S(1)}, bf16[8192,512]{1,0:T(8,128)(2,1)S(1)}, bf16[8192,512]{1,0:T(8,128)(2,1)S(1)}) custom-call(s32[38]{0:T(128)S(1)} %concatenate.55.refs_0_.ctl_ref, ...), custom_call_target="tpu_custom_call", output_to_operand_aliasing={{3}: (2, {}), {4}: (3, {}), {1}: (6, {}), {2}: (7, {})} | custom-call | tf_op jit(solution)/shard_map/forward_step/pallas_call | solution.py:122
  33.7 6.2 %collective-permute-done.1.refs_5_ = bf16[16,8192]{1,0:T(8,128)(2,1)S(1)} collective-permute-done((bf16[16,8192]{1,0:T(8,128)(2,1)S(1)}, bf16[16,8192]{1,0:T(8,128)(2,1)S(1)}, u32[]{:S(2)}, u32[]{:S(2)}) %collective-permute-start.1) | collective-permute-done | bytes 262176 | tf_op jit(solution)/shard_map/ppermute | solution.py:373
  39.9 4.0 %forward_step.19 = (bf16[16,8192]{1,0:T(8,128)(2,1)S(1)}, bf16[8,11,16,1024]{3,2,1,0:T(8,128)(2,1)S(1)}, f32[11,16,640]{2,1,0:T(8,128)S(1)}, bf16[8192,512]{1,0:T(8,128)(2,1)S(1)}, bf16[512,8192]{1,0:T(8,128)(2,1)S(1)}) custom-call(s32[38]{0:T(128)S(1)} %concatenate.55.refs_0_.ctl_ref, ...), custom_call_target="tpu_custom_call", output_to_operand_aliasing={{3}: (2, {}), {4}: (3, {}), {1}: (6, {}), {2}: (7, {})} | custom-call | tf_op jit(solution)/shard_map/forward_step/pallas_call | solution.py:122
  44.1 7.7 %collective-permute-done.2.refs_5_ = bf16[16,8192]{1,0:T(8,128)(2,1)S(1)} collective-permute-done((bf16[16,8192]{1,0:T(8,128)(2,1)S(1)}, bf16[16,8192]{1,0:T(8,128)(2,1)S(1)}, u32[]{:S(2)}, u32[]{:S(2)}) %collective-permute-start.2) | collective-permute-done | bytes 262176 | tf_op jit(solution)/shard_map/ppermute | solution.py:373
  51.8 4.5 %forward_step.20 = (bf16[16,8192]{1,0:T(8,128)(2,1)S(1)}, bf16[8,11,16,1024]{3,2,1,0:T(8,128)(2,1)S(1)}, f32[11,16,640]{2,1,0:T(8,128)S(1)}, bf16[8192,512]{1,0:T(8,128)(2,1)S(1)}, bf16[512,8192]{1,0:T(8,128)(2,1)S(1)}) custom-call(s32[38]{0:T(128)S(1)} %concatenate.55.refs_0_.ctl_ref, ...), custom_call_target="tpu_custom_call", output_to_operand_aliasing={{3}: (2, {}), {4}: (3, {}), {1}: (6, {}), {2}: (7, {})} | custom-call | tf_op jit(solution)/shard_map/forward_step/pallas_call | solution.py:122
  56.4 7.3 %collective-permute-done.3.refs_5_ = bf16[16,8192]{1,0:T(8,128)(2,1)S(1)} collective-permute-done((bf16[16,8192]{1,0:T(8,128)(2,1)S(1)}, bf16[16,8192]{1,0:T(8,128)(2,1)S(1)}, u32[]{:S(2)}, u32[]{:S(2)}) %collective-permute-start.3) | collective-permute-done | bytes 262176 | tf_op jit(solution)/shard_map/ppermute | solution.py:373
  63.7 4.0 %forward_step.21 = (bf16[16,8192]{1,0:T(8,128)(2,1)S(1)}, bf16[8,11,16,1024]{3,2,1,0:T(8,128)(2,1)S(1)}, f32[11,16,640]{2,1,0:T(8,128)S(1)}, bf16[8192,512]{1,0:T(8,128)(2,1)S(1)}, bf16[512,8192]{1,0:T(8,128)(2,1)S(1)}) custom-call(s32[38]{0:T(128)S(1)} %concatenate.55.refs_0_.ctl_ref, ...), custom_call_target="tpu_custom_call", output_to_operand_aliasing={{3}: (2, {}), {4}: (3, {}), {1}: (6, {}), {2}: (7, {})} | custom-call | tf_op jit(solution)/shard_map/forward_step/pallas_call | solution.py:122
  67.8 7.3 %collective-permute-done.4.refs_5_ = bf16[16,8192]{1,0:T(8,128)(2,1)S(1)} collective-permute-done((bf16[16,8192]{1,0:T(8,128)(2,1)S(1)}, bf16[16,8192]{1,0:T(8,128)(2,1)S(1)}, u32[]{:S(2)}, u32[]{:S(2)}) %collective-permute-start.4) | collective-permute-done | bytes 262176 | tf_op jit(solution)/shard_map/ppermute | solution.py:373
  79.3 7.3 %collective-permute-done.5.refs_5_ = bf16[16,8192]{1,0:T(8,128)(2,1)S(1)} collective-permute-done((bf16[16,8192]{1,0:T(8,128)(2,1)S(1)}, bf16[16,8192]{1,0:T(8,128)(2,1)S(1)}, u32[]{:S(2)}, u32[]{:S(2)}) %collective-permute-start.5) | collective-permute-done | bytes 262176 | tf_op jit(solution)/shard_map/ppermute | solution.py:373
  90.7 7.3 %collective-permute-done.6.refs_5_ = bf16[16,8192]{1,0:T(8,128)(2,1)S(1)} collective-permute-done((bf16[16,8192]{1,0:T(8,128)(2,1)S(1)}, bf16[16,8192]{1,0:T(8,128)(2,1)S(1)}, u32[]{:S(2)}, u32[]{:S(2)}) %collective-permute-start.6) | collective-permute-done | bytes 262176 | tf_op jit(solution)/shard_map/ppermute | solution.py:373
  109.9 4.0 %forward_step.25 = (bf16[16,8192]{1,0:T(8,128)(2,1)S(1)}, bf16[8,11,16,1024]{3,2,1,0:T(8,128)(2,1)S(1)}, f32[11,16,640]{2,1,0:T(8,128)S(1)}, bf16[8192,512]{1,0:T(8,128)(2,1)S(1)}, bf16[512,8192]{1,0:T(8,128)(2,1)S(1)}) custom-call(s32[38]{0:T(128)S(1)} %concatenate.55.refs_0_.ctl_ref, ...), custom_call_target="tpu_custom_call", output_to_operand_aliasing={{3}: (2, {}), {4}: (3, {}), {1}: (6, {}), {2}: (7, {})} | custom-call | tf_op jit(solution)/shard_map/forward_step/pallas_call | solution.py:122
  117.0 4.5 %collective-permute-start.10 = (bf16[16,8192]{1,0:T(8,128)(2,1)S(1)}, bf16[16,8192]{1,0:T(8,128)(2,1)S(1)}, u32[]{:S(2)}, u32[]{:S(2)}) collective-permute-start(bf16[16,8192]{1,0:T(8,128)(2,1)S(1)} %get-tuple-element.300), channel_id=1, source_target_pairs={{1,0},{2,1},{3,2},{4,3},{5,4},{6,5},{7,6},{0,7},{9,8},{10,9},{11,1... | collective-permute-start | bytes 786440 | tf_op jit(solution)/shard_map/ppermute | solution.py:389
  121.5 4.0 %forward_step.26 = (bf16[16,8192]{1,0:T(8,128)(2,1)S(1)}, bf16[8,11,16,1024]{3,2,1,0:T(8,128)(2,1)S(1)}, f32[11,16,640]{2,1,0:T(8,128)S(1)}, bf16[8192,512]{1,0:T(8,128)(2,1)S(1)}, bf16[512,8192]{1,0:T(8,128)(2,1)S(1)}) custom-call(s32[38]{0:T(128)S(1)} %concatenate.55.refs_0_.ctl_ref, ...), custom_call_target="tpu_custom_call", output_to_operand_aliasing={{3}: (2, {}), {4}: (3, {}), {1}: (6, {}), {2}: (7, {})} | custom-call | tf_op jit(solution)/shard_map/forward_step/pallas_call | solution.py:122
  128.7 4.8 %collective-permute-start.12 = (bf16[16,8192]{1,0:T(8,128)(2,1)S(1)}, bf16[16,8192]{1,0:T(8,128)(2,1)S(1)}, u32[]{:S(2)}, u32[]{:S(2)}) collective-permute-start(bf16[16,8192]{1,0:T(8,128)(2,1)S(1)} %get-tuple-element.312), channel_id=1, source_target_pairs={{1,0},{2,1},{3,2},{4,3},{5,4},{6,5},{7,6},{0,7},{9,8},{10,9},{11,1... | collective-permute-start | bytes 786440 | tf_op jit(solution)/shard_map/ppermute | solution.py:389
  140.0 5.0 %collective-permute-start.14 = (bf16[16,8192]{1,0:T(8,128)(2,1)S(1)}, bf16[16,8192]{1,0:T(8,128)(2,1)S(1)}, u32[]{:S(2)}, u32[]{:S(2)}) collective-permute-start(bf16[16,8192]{1,0:T(8,128)(2,1)S(1)} %get-tuple-element.324), channel_id=1, source_target_pairs={{1,0},{2,1},{3,2},{4,3},{5,4},{6,5},{7,6},{0,7},{9,8},{10,9},{11,1... | collective-permute-start | bytes 786440 | tf_op jit(solution)/shard_map/ppermute | solution.py:389
  152.9 5.0 %collective-permute-start.16 = (bf16[16,8192]{1,0:T(8,128)(2,1)S(1)}, bf16[16,8192]{1,0:T(8,128)(2,1)S(1)}, u32[]{:S(2)}, u32[]{:S(2)}) collective-permute-start(bf16[16,8192]{1,0:T(8,128)(2,1)S(1)} %get-tuple-element.336), channel_id=1, source_target_pairs={{1,0},{2,1},{3,2},{4,3},{5,4},{6,5},{7,6},{0,7},{9,8},{10,9},{11,1... | collective-permute-start | bytes 786440 | tf_op jit(solution)/shard_map/ppermute | solution.py:389
  167.4 5.3 %collective-permute-start.18 = (bf16[16,8192]{1,0:T(8,128)(2,1)S(1)}, bf16[16,8192]{1,0:T(8,128)(2,1)S(1)}, u32[]{:S(2)}, u32[]{:S(2)}) collective-permute-start(bf16[16,8192]{1,0:T(8,128)(2,1)S(1)} %get-tuple-element.348), channel_id=1, source_target_pairs={{1,0},{2,1},{3,2},{4,3},{5,4},{6,5},{7,6},{0,7},{9,8},{10,9},{11,1... | collective-permute-start | bytes 786440 | tf_op jit(solution)/shard_map/ppermute | solution.py:389
  181.4 5.3 %collective-permute-start.20 = (bf16[16,8192]{1,0:T(8,128)(2,1)S(1)}, bf16[16,8192]{1,0:T(8,128)(2,1)S(1)}, u32[]{:S(2)}, u32[]{:S(2)}) collective-permute-start(bf16[16,8192]{1,0:T(8,128)(2,1)S(1)} %get-tuple-element.360), channel_id=1, source_target_pairs={{1,0},{2,1},{3,2},{4,3},{5,4},{6,5},{7,6},{0,7},{9,8},{10,9},{11,1... | collective-permute-start | bytes 786440 | tf_op jit(solution)/shard_map/ppermute | solution.py:389
  194.1 5.5 %collective-permute-start.22 = (bf16[16,8192]{1,0:T(8,128)(2,1)S(1)}, bf16[16,8192]{1,0:T(8,128)(2,1)S(1)}, u32[]{:S(2)}, u32[]{:S(2)}) collective-permute-start(bf16[16,8192]{1,0:T(8,128)(2,1)S(1)} %get-tuple-element.372), channel_id=1, source_target_pairs={{1,0},{2,1},{3,2},{4,3},{5,4},{6,5},{7,6},{0,7},{9,8},{10,9},{11,1... | collective-permute-start | bytes 786440 | tf_op jit(solution)/shard_map/ppermute | solution.py:389
  206.2 5.3 %collective-permute-start.24 = (bf16[16,8192]{1,0:T(8,128)(2,1)S(1)}, bf16[16,8192]{1,0:T(8,128)(2,1)S(1)}, u32[]{:S(2)}, u32[]{:S(2)}) collective-permute-start(bf16[16,8192]{1,0:T(8,128)(2,1)S(1)} %get-tuple-element.384), channel_id=1, source_target_pairs={{1,0},{2,1},{3,2},{4,3},{5,4},{6,5},{7,6},{0,7},{9,8},{10,9},{11,1... | collective-permute-start | bytes 786440 | tf_op jit(solution)/shard_map/ppermute | solution.py:389
  219.3 4.9 %collective-permute-start.25 = (bf16[16,8192]{1,0:T(8,128)(2,1)S(1)}, bf16[16,8192]{1,0:T(8,128)(2,1)S(1)}, u32[]{:S(2)}, u32[]{:S(2)}) collective-permute-start(bf16[16,8192]{1,0:T(8,128)(2,1)S(1)} %get-tuple-element.391), channel_id=1, source_target_pairs={{1,0},{2,1},{3,2},{4,3},{5,4},{6,5},{7,6},{0,7},{9,8},{10,9},{11,1... | collective-permute-start | bytes 786440 | tf_op jit(solution)/shard_map/ppermute | solution.py:389
  230.5 4.1 %collective-permute-start.26 = (bf16[16,8192]{1,0:T(8,128)(2,1)S(1)}, bf16[16,8192]{1,0:T(8,128)(2,1)S(1)}, u32[]{:S(2)}, u32[]{:S(2)}) collective-permute-start(bf16[16,8192]{1,0:T(8,128)(2,1)S(1)} %get-tuple-element.394), channel_id=1, source_target_pairs={{1,0},{2,1},{3,2},{4,3},{5,4},{6,5},{7,6},{0,7},{9,8},{10,9},{11,1... | collective-permute-start | bytes 786440 | tf_op jit(solution)/shard_map/ppermute | solution.py:389
  240.9 4.1 %collective-permute-start.28 = (bf16[16,8192]{1,0:T(8,128)(2,1)S(1)}, bf16[16,8192]{1,0:T(8,128)(2,1)S(1)}, u32[]{:S(2)}, u32[]{:S(2)}) collective-permute-start(bf16[16,8192]{1,0:T(8,128)(2,1)S(1)} %get-tuple-element.404), channel_id=1, source_target_pairs={{1,0},{2,1},{3,2},{4,3},{5,4},{6,5},{7,6},{0,7},{9,8},{10,9},{11,1... | collective-permute-start | bytes 786440 | tf_op jit(solution)/shard_map/ppermute | solution.py:389
  247.7 4.6 %collective-permute-done.29.refs_2_ = bf16[320,1024]{1,0:T(8,128)(2,1)S(1)} collective-permute-done((bf16[320,1024]{1,0:T(8,128)(2,1)S(1)}, bf16[320,1024]{1,0:T(8,128)(2,1)S(1)}, u32[]{:S(2)}, u32[]{:S(2)}) %collective-permute-start.29) | collective-permute-done | bytes 655392 | tf_op jit(solution)/shard_map/ppermute | solution.py:341
  266.7 7.7 %collective-permute-start.36 = (bf16[192,1024]{1,0:T(8,128)(2,1)S(1)}, bf16[192,1024]{1,0:T(8,128)(2,1)S(1)}, u32[]{:S(2)}, u32[]{:S(2)}) collective-permute-start(bf16[192,1024]{1,0:T(8,128)(2,1)S(1)} %pad_maximum_fusion.10), channel_id=1, source_target_pairs={{0,48},{16,32},{32,16},{48,0},{1,49},{17,33},{33,17},{49,1},{2,50}... | collective-permute-start | bytes 1179656 | tf_op jit(solution)/shard_map/ppermute | solution.py:341
  281.2 4.5 %collective-permute-start.38 = (bf16[192,1024]{1,0:T(8,128)(2,1)S(1)}, bf16[192,1024]{1,0:T(8,128)(2,1)S(1)}, u32[]{:S(2)}, u32[]{:S(2)}) collective-permute-start(bf16[192,1024]{1,0:T(8,128)(2,1)S(1)} %get-tuple-element.496), channel_id=1, source_target_pairs={{0,16},{16,0},{32,48},{48,32},{1,17},{17,1},{33,49},{49,33},{2,18}... | collective-permute-start | bytes 1179656 | tf_op jit(solution)/shard_map/ppermute | solution.py:341
  308.7 10.5 %gradient_step.1 = (f32[2,512,512]{2,1,0:T(8,128)S(1)}, bf16[2,512,512]{2,1,0:T(8,128)(2,1)S(1)}, f32[2,512,512]{2,1,0:T(8,128)S(1)}, bf16[2,512,512]{2,1,0:T(8,128)(2,1)S(1)}) custom-call(s32[38]{0:T(128)S(1)} %concatenate.55.refs_0_.ctl_ref, bf16[320,1024]{1,0:T(8,128)(2,1)S(1)} %pad_maximum_fusion.refs_0_, ...), custom_call_target="tpu_custom_call" | custom-call | tf_op jit(solution)/shard_map/gradient_step/pallas_call | solution.py:275
  319.2 24.8 %collective-permute-start.46 = (bf16[2,512,512]{2,1,0:T(8,128)(2,1)S(1)}, bf16[2,512,512]{2,1,0:T(8,128)(2,1)S(1)}, u32[]{:S(2)}, u32[]{:S(2)}) collective-permute-start(bf16[2,512,512]{2,1,0:T(8,128)(2,1)S(1)} %get-tuple-element.461), channel_id=1, source_target_pairs={{0,8},{8,0},{1,9},{9,1},{2,10},{10,2},{3,11},{11,3},{4,12},{12,4},... | collective-permute-start | bytes 3145736 | tf_op jit(solution)/shard_map/ppermute | solution.py:403
  350.5 10.7 %collective-permute-done.47 = bf16[512,512]{1,0:T(8,128)(2,1)S(1)} collective-permute-done((bf16[512,512]{1,0:T(8,128)(2,1)S(1)}, bf16[512,512]{1,0:T(8,128)(2,1)S(1)}, u32[]{:S(2)}, u32[]{:S(2)}) %collective-permute-start.47) | collective-permute-done | bytes 524320 | tf_op jit(solution)/shard_map/ppermute | solution.py:405
  362.4 10.1 %collective-permute-done.45.far_ref = bf16[512,512]{1,0:T(8,128)(2,1)S(1)} collective-permute-done((bf16[512,512]{1,0:T(8,128)(2,1)S(1)}, bf16[512,512]{1,0:T(8,128)(2,1)S(1)}, u32[]{:S(2)}, u32[]{:S(2)}) %collective-permute-start.45) | collective-permute-done | bytes 524320 | tf_op jit(solution)/shard_map/ppermute | solution.py:405
  (140 shorter events, 159.7 us)
Async XLA Ops:
  14.4 11.6 %collective-permute-start = (bf16[16,8192]{1,0:T(8,128)(2,1)S(1)}, bf16[16,8192]{1,0:T(8,128)(2,1)S(1)}, u32[]{:S(2)}, u32[]{:S(2)}) collective-permute-start(bf16[16,8192]{1,0:T(8,128)(2,1)S(1)} %get-tuple-element.241), channel_id=1, source_target_pairs={{0,1},{1,2},{2,3},{3,4},{4,5},{5,6},{6,7},{7,0},{8,9},{9,10},{10,1... | collective-permute-start | bytes 786440 | tf_op jit(solution)/shard_map/ppermute | solution.py:373
  31.2 8.8 %collective-permute-start.1 = (bf16[16,8192]{1,0:T(8,128)(2,1)S(1)}, bf16[16,8192]{1,0:T(8,128)(2,1)S(1)}, u32[]{:S(2)}, u32[]{:S(2)}) collective-permute-start(bf16[16,8192]{1,0:T(8,128)(2,1)S(1)} %get-tuple-element.249), channel_id=1, source_target_pairs={{0,1},{1,2},{2,3},{3,4},{4,5},{5,6},{6,7},{7,0},{8,9},{9,10},{10,1... | collective-permute-start | bytes 786440 | tf_op jit(solution)/shard_map/ppermute | solution.py:373
  117.0 8.7 %collective-permute-start.10 = (bf16[16,8192]{1,0:T(8,128)(2,1)S(1)}, bf16[16,8192]{1,0:T(8,128)(2,1)S(1)}, u32[]{:S(2)}, u32[]{:S(2)}) collective-permute-start(bf16[16,8192]{1,0:T(8,128)(2,1)S(1)} %get-tuple-element.300), channel_id=1, source_target_pairs={{1,0},{2,1},{3,2},{4,3},{5,4},{6,5},{7,6},{0,7},{9,8},{10,9},{11,1... | collective-permute-start | bytes 786440 | tf_op jit(solution)/shard_map/ppermute | solution.py:389
  136.5 9.4 %collective-permute-start.13 = (bf16[16,8192]{1,0:T(8,128)(2,1)S(1)}, bf16[16,8192]{1,0:T(8,128)(2,1)S(1)}, u32[]{:S(2)}, u32[]{:S(2)}) collective-permute-start(bf16[16,8192]{1,0:T(8,128)(2,1)S(1)} %get-tuple-element.319), channel_id=1, source_target_pairs={{0,1},{1,2},{2,3},{3,4},{4,5},{5,6},{6,7},{7,0},{8,9},{9,10},{10,1... | collective-permute-start | bytes 786440 | tf_op jit(solution)/shard_map/ppermute | solution.py:373
  140.0 10.0 %collective-permute-start.14 = (bf16[16,8192]{1,0:T(8,128)(2,1)S(1)}, bf16[16,8192]{1,0:T(8,128)(2,1)S(1)}, u32[]{:S(2)}, u32[]{:S(2)}) collective-permute-start(bf16[16,8192]{1,0:T(8,128)(2,1)S(1)} %get-tuple-element.324), channel_id=1, source_target_pairs={{1,0},{2,1},{3,2},{4,3},{5,4},{6,5},{7,6},{0,7},{9,8},{10,9},{11,1... | collective-permute-start | bytes 786440 | tf_op jit(solution)/shard_map/ppermute | solution.py:389
  149.1 10.2 %collective-permute-start.15 = (bf16[16,8192]{1,0:T(8,128)(2,1)S(1)}, bf16[16,8192]{1,0:T(8,128)(2,1)S(1)}, u32[]{:S(2)}, u32[]{:S(2)}) collective-permute-start(bf16[16,8192]{1,0:T(8,128)(2,1)S(1)} %get-tuple-element.331), channel_id=1, source_target_pairs={{0,1},{1,2},{2,3},{3,4},{4,5},{5,6},{6,7},{7,0},{8,9},{9,10},{10,1... | collective-permute-start | bytes 786440 | tf_op jit(solution)/shard_map/ppermute | solution.py:373
  152.9 11.1 %collective-permute-start.16 = (bf16[16,8192]{1,0:T(8,128)(2,1)S(1)}, bf16[16,8192]{1,0:T(8,128)(2,1)S(1)}, u32[]{:S(2)}, u32[]{:S(2)}) collective-permute-start(bf16[16,8192]{1,0:T(8,128)(2,1)S(1)} %get-tuple-element.336), channel_id=1, source_target_pairs={{1,0},{2,1},{3,2},{4,3},{5,4},{6,5},{7,6},{0,7},{9,8},{10,9},{11,1... | collective-permute-start | bytes 786440 | tf_op jit(solution)/shard_map/ppermute | solution.py:389
  162.3 10.4 %collective-permute-start.17 = (bf16[16,8192]{1,0:T(8,128)(2,1)S(1)}, bf16[16,8192]{1,0:T(8,128)(2,1)S(1)}, u32[]{:S(2)}, u32[]{:S(2)}) collective-permute-start(bf16[16,8192]{1,0:T(8,128)(2,1)S(1)} %get-tuple-element.343), channel_id=1, source_target_pairs={{0,1},{1,2},{2,3},{3,4},{4,5},{5,6},{6,7},{7,0},{8,9},{9,10},{10,1... | collective-permute-start | bytes 786440 | tf_op jit(solution)/shard_map/ppermute | solution.py:373
  167.4 11.0 %collective-permute-start.18 = (bf16[16,8192]{1,0:T(8,128)(2,1)S(1)}, bf16[16,8192]{1,0:T(8,128)(2,1)S(1)}, u32[]{:S(2)}, u32[]{:S(2)}) collective-permute-start(bf16[16,8192]{1,0:T(8,128)(2,1)S(1)} %get-tuple-element.348), channel_id=1, source_target_pairs={{1,0},{2,1},{3,2},{4,3},{5,4},{6,5},{7,6},{0,7},{9,8},{10,9},{11,1... | collective-permute-start | bytes 786440 | tf_op jit(solution)/shard_map/ppermute | solution.py:389
  175.8 10.9 %collective-permute-start.19 = (bf16[16,8192]{1,0:T(8,128)(2,1)S(1)}, bf16[16,8192]{1,0:T(8,128)(2,1)S(1)}, u32[]{:S(2)}, u32[]{:S(2)}) collective-permute-start(bf16[16,8192]{1,0:T(8,128)(2,1)S(1)} %get-tuple-element.355), channel_id=1, source_target_pairs={{0,1},{1,2},{2,3},{3,4},{4,5},{5,6},{6,7},{7,0},{8,9},{9,10},{10,1... | collective-permute-start | bytes 786440 | tf_op jit(solution)/shard_map/ppermute | solution.py:373
  181.4 9.7 %collective-permute-start.20 = (bf16[16,8192]{1,0:T(8,128)(2,1)S(1)}, bf16[16,8192]{1,0:T(8,128)(2,1)S(1)}, u32[]{:S(2)}, u32[]{:S(2)}) collective-permute-start(bf16[16,8192]{1,0:T(8,128)(2,1)S(1)} %get-tuple-element.360), channel_id=1, source_target_pairs={{1,0},{2,1},{3,2},{4,3},{5,4},{6,5},{7,6},{0,7},{9,8},{10,9},{11,1... | collective-permute-start | bytes 786440 | tf_op jit(solution)/shard_map/ppermute | solution.py:389
  189.8 9.8 %collective-permute-start.21 = (bf16[16,8192]{1,0:T(8,128)(2,1)S(1)}, bf16[16,8192]{1,0:T(8,128)(2,1)S(1)}, u32[]{:S(2)}, u32[]{:S(2)}) collective-permute-start(bf16[16,8192]{1,0:T(8,128)(2,1)S(1)} %get-tuple-element.367), channel_id=1, source_target_pairs={{0,1},{1,2},{2,3},{3,4},{4,5},{5,6},{6,7},{7,0},{8,9},{9,10},{10,1... | collective-permute-start | bytes 786440 | tf_op jit(solution)/shard_map/ppermute | solution.py:373
  194.1 9.1 %collective-permute-start.22 = (bf16[16,8192]{1,0:T(8,128)(2,1)S(1)}, bf16[16,8192]{1,0:T(8,128)(2,1)S(1)}, u32[]{:S(2)}, u32[]{:S(2)}) collective-permute-start(bf16[16,8192]{1,0:T(8,128)(2,1)S(1)} %get-tuple-element.372), channel_id=1, source_target_pairs={{1,0},{2,1},{3,2},{4,3},{5,4},{6,5},{7,6},{0,7},{9,8},{10,9},{11,1... | collective-permute-start | bytes 786440 | tf_op jit(solution)/shard_map/ppermute | solution.py:389
  202.7 8.8 %collective-permute-start.23 = (bf16[16,8192]{1,0:T(8,128)(2,1)S(1)}, bf16[16,8192]{1,0:T(8,128)(2,1)S(1)}, u32[]{:S(2)}, u32[]{:S(2)}) collective-permute-start(bf16[16,8192]{1,0:T(8,128)(2,1)S(1)} %get-tuple-element.379), channel_id=1, source_target_pairs={{0,1},{1,2},{2,3},{3,4},{4,5},{5,6},{6,7},{7,0},{8,9},{9,10},{10,1... | collective-permute-start | bytes 786440 | tf_op jit(solution)/shard_map/ppermute | solution.py:373
  206.2 8.6 %collective-permute-start.24 = (bf16[16,8192]{1,0:T(8,128)(2,1)S(1)}, bf16[16,8192]{1,0:T(8,128)(2,1)S(1)}, u32[]{:S(2)}, u32[]{:S(2)}) collective-permute-start(bf16[16,8192]{1,0:T(8,128)(2,1)S(1)} %get-tuple-element.384), channel_id=1, source_target_pairs={{1,0},{2,1},{3,2},{4,3},{5,4},{6,5},{7,6},{0,7},{9,8},{10,9},{11,1... | collective-permute-start | bytes 786440 | tf_op jit(solution)/shard_map/ppermute | solution.py:389
  218.0 20.0 %collective-permute-start.27 = (bf16[320,1024]{1,0:T(8,128)(2,1)S(1)}, bf16[320,1024]{1,0:T(8,128)(2,1)S(1)}, u32[]{:S(2)}, u32[]{:S(2)}) collective-permute-start(bf16[320,1024]{1,0:T(8,128)(2,1)S(1)} %pad_maximum_fusion.1), channel_id=1, source_target_pairs={{0,16},{16,0},{32,48},{48,32},{1,17},{17,1},{33,49},{49,33},{2,18}... | collective-permute-start | bytes 1966088 | tf_op jit(solution)/shard_map/ppermute | solution.py:341
  234.7 17.5 %collective-permute-start.29 = (bf16[320,1024]{1,0:T(8,128)(2,1)S(1)}, bf16[320,1024]{1,0:T(8,128)(2,1)S(1)}, u32[]{:S(2)}, u32[]{:S(2)}) collective-permute-start(bf16[320,1024]{1,0:T(8,128)(2,1)S(1)} %pad_maximum_fusion.2), channel_id=1, source_target_pairs={{0,32},{16,48},{32,0},{48,16},{1,33},{17,49},{33,1},{49,17},{2,34}... | collective-permute-start | bytes 1966088 | tf_op jit(solution)/shard_map/ppermute | solution.py:341
  240.9 11.4 %collective-permute-start.28 = (bf16[16,8192]{1,0:T(8,128)(2,1)S(1)}, bf16[16,8192]{1,0:T(8,128)(2,1)S(1)}, u32[]{:S(2)}, u32[]{:S(2)}) collective-permute-start(bf16[16,8192]{1,0:T(8,128)(2,1)S(1)} %get-tuple-element.404), channel_id=1, source_target_pairs={{1,0},{2,1},{3,2},{4,3},{5,4},{6,5},{7,6},{0,7},{9,8},{10,9},{11,1... | collective-permute-start | bytes 786440 | tf_op jit(solution)/shard_map/ppermute | solution.py:389
  245.1 15.7 %collective-permute-start.31 = (bf16[320,1024]{1,0:T(8,128)(2,1)S(1)}, bf16[320,1024]{1,0:T(8,128)(2,1)S(1)}, u32[]{:S(2)}, u32[]{:S(2)}) collective-permute-start(bf16[320,1024]{1,0:T(8,128)(2,1)S(1)} %pad_maximum_fusion.3), channel_id=1, source_target_pairs={{0,48},{16,32},{32,16},{48,0},{1,49},{17,33},{33,17},{49,1},{2,50}... | collective-permute-start | bytes 1966088 | tf_op jit(solution)/shard_map/ppermute | solution.py:341
  247.2 10.9 %collective-permute-start.32 = (bf16[192,1024]{1,0:T(8,128)(2,1)S(1)}, bf16[192,1024]{1,0:T(8,128)(2,1)S(1)}, u32[]{:S(2)}, u32[]{:S(2)}) collective-permute-start(bf16[192,1024]{1,0:T(8,128)(2,1)S(1)} %get-tuple-element.498), channel_id=1, source_target_pairs={{0,16},{16,0},{32,48},{48,32},{1,17},{17,1},{33,49},{49,33},{2,18}... | collective-permute-start | bytes 1179656 | tf_op jit(solution)/shard_map/ppermute | solution.py:341
  255.4 19.0 %collective-permute-start.34 = (bf16[192,1024]{1,0:T(8,128)(2,1)S(1)}, bf16[192,1024]{1,0:T(8,128)(2,1)S(1)}, u32[]{:S(2)}, u32[]{:S(2)}) collective-permute-start(bf16[192,1024]{1,0:T(8,128)(2,1)S(1)} %pad_maximum_fusion.9), channel_id=1, source_target_pairs={{0,32},{16,48},{32,0},{48,16},{1,33},{17,49},{33,1},{49,17},{2,34}... | collective-permute-start | bytes 1179656 | tf_op jit(solution)/shard_map/ppermute | solution.py:341
  263.8 10.6 %collective-permute-start.33 = (bf16[16,8192]{1,0:T(8,128)(2,1)S(1)}, bf16[16,8192]{1,0:T(8,128)(2,1)S(1)}, u32[]{:S(2)}, u32[]{:S(2)}) collective-permute-start(bf16[16,8192]{1,0:T(8,128)(2,1)S(1)} %get-tuple-element.424), channel_id=1, source_target_pairs={{1,0},{2,1},{3,2},{4,3},{5,4},{6,5},{7,6},{0,7},{9,8},{10,9},{11,1... | collective-permute-start | bytes 786440 | tf_op jit(solution)/shard_map/ppermute | solution.py:389
  266.7 19.1 %collective-permute-start.36 = (bf16[192,1024]{1,0:T(8,128)(2,1)S(1)}, bf16[192,1024]{1,0:T(8,128)(2,1)S(1)}, u32[]{:S(2)}, u32[]{:S(2)}) collective-permute-start(bf16[192,1024]{1,0:T(8,128)(2,1)S(1)} %pad_maximum_fusion.10), channel_id=1, source_target_pairs={{0,48},{16,32},{32,16},{48,0},{1,49},{17,33},{33,17},{49,1},{2,50}... | collective-permute-start | bytes 1179656 | tf_op jit(solution)/shard_map/ppermute | solution.py:341
  277.3 8.4 %collective-permute-start.35 = (bf16[16,8192]{1,0:T(8,128)(2,1)S(1)}, bf16[16,8192]{1,0:T(8,128)(2,1)S(1)}, u32[]{:S(2)}, u32[]{:S(2)}) collective-permute-start(bf16[16,8192]{1,0:T(8,128)(2,1)S(1)} %get-tuple-element.433), channel_id=1, source_target_pairs={{1,0},{2,1},{3,2},{4,3},{5,4},{6,5},{7,6},{0,7},{9,8},{10,9},{11,1... | collective-permute-start | bytes 786440 | tf_op jit(solution)/shard_map/ppermute | solution.py:389
  278.5 16.7 %collective-permute-start.39 = (bf16[192,1024]{1,0:T(8,128)(2,1)S(1)}, bf16[192,1024]{1,0:T(8,128)(2,1)S(1)}, u32[]{:S(2)}, u32[]{:S(2)}) collective-permute-start(bf16[192,1024]{1,0:T(8,128)(2,1)S(1)} %get-tuple-element.495), channel_id=1, source_target_pairs={{0,32},{16,48},{32,0},{48,16},{1,33},{17,49},{33,1},{49,17},{2,34}... | collective-permute-start | bytes 1179656 | tf_op jit(solution)/shard_map/ppermute | solution.py:341
  281.2 14.0 %collective-permute-start.38 = (bf16[192,1024]{1,0:T(8,128)(2,1)S(1)}, bf16[192,1024]{1,0:T(8,128)(2,1)S(1)}, u32[]{:S(2)}, u32[]{:S(2)}) collective-permute-start(bf16[192,1024]{1,0:T(8,128)(2,1)S(1)} %get-tuple-element.496), channel_id=1, source_target_pairs={{0,16},{16,0},{32,48},{48,32},{1,17},{17,1},{33,49},{49,33},{2,18}... | collective-permute-start | bytes 1179656 | tf_op jit(solution)/shard_map/ppermute | solution.py:341
  288.7 8.4 %collective-permute-start.37 = (bf16[16,8192]{1,0:T(8,128)(2,1)S(1)}, bf16[16,8192]{1,0:T(8,128)(2,1)S(1)}, u32[]{:S(2)}, u32[]{:S(2)}) collective-permute-start(bf16[16,8192]{1,0:T(8,128)(2,1)S(1)} %get-tuple-element.442), channel_id=1, source_target_pairs={{1,0},{2,1},{3,2},{4,3},{5,4},{6,5},{7,6},{0,7},{9,8},{10,9},{11,1... | collective-permute-start | bytes 786440 | tf_op jit(solution)/shard_map/ppermute | solution.py:389
  291.5 13.1 %collective-permute-start.40 = (bf16[192,1024]{1,0:T(8,128)(2,1)S(1)}, bf16[192,1024]{1,0:T(8,128)(2,1)S(1)}, u32[]{:S(2)}, u32[]{:S(2)}) collective-permute-start(bf16[192,1024]{1,0:T(8,128)(2,1)S(1)} %pad_maximum_fusion.11), channel_id=1, source_target_pairs={{0,48},{16,32},{32,16},{48,0},{1,49},{17,33},{33,17},{49,1},{2,50}... | collective-permute-start | bytes 1179656 | tf_op jit(solution)/shard_map/ppermute | solution.py:341
  299.0 9.7 %collective-permute-start.43 = (bf16[96,1024]{1,0:T(8,128)(2,1)S(1)}, bf16[96,1024]{1,0:T(8,128)(2,1)S(1)}, u32[]{:S(2)}, u32[]{:S(2)}) collective-permute-start(bf16[96,1024]{1,0:T(8,128)(2,1)S(1)} %get-tuple-element.500), channel_id=1, source_target_pairs={{0,48},{16,32},{32,16},{48,0},{1,49},{17,33},{33,17},{49,1},{2,50}... | collective-permute-start | bytes 589832 | tf_op jit(solution)/shard_map/ppermute | solution.py:341
  319.2 27.1 %collective-permute-start.46 = (bf16[2,512,512]{2,1,0:T(8,128)(2,1)S(1)}, bf16[2,512,512]{2,1,0:T(8,128)(2,1)S(1)}, u32[]{:S(2)}, u32[]{:S(2)}) collective-permute-start(bf16[2,512,512]{2,1,0:T(8,128)(2,1)S(1)} %get-tuple-element.461), channel_id=1, source_target_pairs={{0,8},{8,0},{1,9},{9,1},{2,10},{10,2},{3,11},{11,3},{4,12},{12,4},... | collective-permute-start | bytes 3145736 | tf_op jit(solution)/shard_map/ppermute | solution.py:403
  346.5 14.7 %collective-permute-start.47 = (bf16[512,512]{1,0:T(8,128)(2,1)S(1)}, bf16[512,512]{1,0:T(8,128)(2,1)S(1)}, u32[]{:S(2)}, u32[]{:S(2)}) collective-permute-start(bf16[512,512]{1,0:T(8,128)(2,1)S(1)} %fusion.2), channel_id=1, source_target_pairs={{0,64},{64,0},{1,65},{65,1},{2,66},{66,2},{3,67},{67,3},{4,68},{68... | collective-permute-start | bytes 1572872 | tf_op jit(solution)/shard_map/ppermute | solution.py:405
  349.2 23.2 %collective-permute-start.45 = (bf16[512,512]{1,0:T(8,128)(2,1)S(1)}, bf16[512,512]{1,0:T(8,128)(2,1)S(1)}, u32[]{:S(2)}, u32[]{:S(2)}) collective-permute-start(bf16[512,512]{1,0:T(8,128)(2,1)S(1)} %fusion.1), channel_id=1, source_target_pairs={{0,64},{64,0},{1,65},{65,1},{2,66},{66,2},{3,67},{67,3},{4,68},{68... | collective-permute-start | bytes 1572872 | tf_op jit(solution)/shard_map/ppermute | solution.py:405
  (18 other events, 127.6 us)
